TPU v7x, 128 devices: a whole 4x4x4 slice. The times are simulated.
128 devices in a mesh: ctx: 32 (over x, z_hi, y), ch: 2 (over z_lo), section: 2 (over core).
Axes of the slice: x: 4, y: 4, z: 4 (z_hi: 2, z_lo: 2; z = z_hi * 2 + z_lo), core: 2. Of those that a mesh axis runs over, the one named last changes fastest.
Arguments:
- mamba_x: bfloat16 [4096, 8192], P('ctx', ('ch', 'section')), may hold values from -6 to 6
- mamba_b: bfloat16 [4096, 1024], P('ctx', ('ch', 'section')), may hold values from -6 to 6
- mamba_c: bfloat16 [4096, 1024], P('ctx', ('ch', 'section')), may hold values from -6 to 6
- step_dt: float32 [4096, 64], P('ctx', ('ch', 'section')), may hold values from 0 to 0.35, as said below
- decay_a: float32 [64], P(('ch', 'section')), may hold values from 0.5 to 2
- skip_d: float32 [64], P(('ch', 'section')), may hold values from 0.5 to 1.5
- value_weight: bfloat16 [8192, 1024], P(('ch', 'section')), may hold values from -0.0625 to 0.0625
- queries: bfloat16 [4096, 8192], P('ctx', ('ch', 'section')), may hold values from -20 to 20
- keys: bfloat16 [4096, 1024], P('ctx', ('ch', 'section')), may hold values from -6 to 6
- out_grad: bfloat16 [4096, 8192], P('ctx', ('ch', 'section')), may hold values from -6 to 6
Outputs:
- attn_out: float32 [4096, 8192], P('ctx', ('ch', 'section'))
- grad_q: float32 [4096, 8192], P('ctx', ('ch', 'section'))
- grad_k: float32 [4096, 1024], P('ctx', ('ch', 'section'))
- grad_x: float32 [4096, 8192], P('ctx', ('ch', 'section'))
- grad_b: float32 [4096, 1024], P('ctx', ('ch', 'section'))
- grad_c: float32 [4096, 1024], P('ctx', ('ch', 'section'))
Inputs may be any that keep to these rules, and one draw needn't show every extreme that they name: `step_dt`: positive step sizes.
All inputs are finite; a program needn't handle non-finite values.
Results may differ from a plain program's by a relative error of at most 0.0059.
Values may be sent and summed in bfloat16 or wider, within the bound.
No kernel may reach another device: no remote copies, remote signals or barrier semaphores. Data moves between devices by JAX's collectives and lax.ppermute only.
A program may use at most 128 MiB of HBM per device.

v0:
```python
import functools
import math

import jax
import jax.numpy as jnp
from jax import lax
from jax.sharding import PartitionSpec as P

HEAD_P = 128
STATE = 128
Q_HEADS = 64
KV_HEADS = 8
HEAD_DIM = 128


HIGHEST = lax.Precision.HIGHEST
NEG_FILL = -1e30


def carried_in(part, axis, combine, identity, reverse):
    count = lax.axis_size(axis)
    place = lax.axis_index(axis)
    ahead = count - 1 - place if reverse else place
    gathered = jax.tree.map(lambda a: lax.all_gather(a, axis), part)
    state = jax.tree.map(lambda a, e: jnp.zeros_like(a) + jnp.asarray(e, a.dtype), part, identity)

    def one(hop, state):
        source = count - 1 - hop if reverse else hop
        return combine(
            state, jax.tree.map(lambda a: lax.dynamic_index_in_dim(a, source, 0, False), gathered)
        )

    return lax.fori_loop(0, ahead, one, state)


def block_terms(inputs_x, inputs_b, inputs_c, step_sizes, decay_rates, skip_gains):
    head_count = inputs_x.shape[1]
    repeat_by = head_count // inputs_b.shape[1]
    log_sums = jnp.cumsum(-step_sizes * decay_rates[None, :], axis=0)
    positions = jnp.arange(log_sums.shape[0])
    lower_mask = (positions[:, None] >= positions[None, :])[None]
    log_gaps = log_sums.T[:, :, None] - log_sums.T[:, None, :]
    decays = jnp.where(lower_mask, jnp.exp(jnp.where(lower_mask, log_gaps, 0.0)), 0.0)
    inner_prod = jnp.einsum("tgn,sgn->gts", inputs_c, inputs_b, precision=HIGHEST)
    inner_prod = jnp.repeat(inner_prod, repeat_by, axis=0)
    mixing = inner_prod * decays * step_sizes.T[:, None, :]
    local_out = (
        jnp.einsum("hts,shp->thp", mixing, inputs_x, precision=HIGHEST)
        + skip_gains[None, :, None] * inputs_x
    )
    to_end = jnp.exp(log_sums[-1][None, :] - log_sums) * step_sizes
    b_heads = jnp.repeat(inputs_b, repeat_by, axis=1)
    weighted = inputs_x * to_end[:, :, None]
    end_state = jnp.einsum("shp,shn->hpn", weighted, b_heads, precision=HIGHEST)
    return (local_out, end_state, jnp.exp(log_sums[-1]))


def entry_terms(inputs_c, step_sizes, decay_rates, entering):
    repeat_by = entering.shape[0] // inputs_c.shape[1]
    log_sums = jnp.cumsum(-step_sizes * decay_rates[None, :], axis=0)
    c_heads = jnp.repeat(inputs_c, repeat_by, axis=1)
    carried = jnp.einsum("thn,hpn->thp", c_heads, entering, precision=HIGHEST)
    return jnp.exp(log_sums)[:, :, None] * carried


def link_states(earlier, later):
    return (earlier[0] * later[0], later[0][:, None, None] * earlier[1] + later[1])


def blockwise(carried_acc, key_piece, value_piece, update):
    segment_length = key_piece.shape[0]
    block_rows = math.gcd(segment_length, 512)

    def advance(block_index, running):
        first_row = block_index * block_rows
        key_tile_rows = lax.dynamic_slice_in_dim(key_piece, first_row, block_rows, 0)
        value_tile_rows = lax.dynamic_slice_in_dim(value_piece, first_row, block_rows, 0)
        return update(running, key_tile_rows, value_tile_rows, first_row)

    return lax.fori_loop(0, segment_length // block_rows, advance, carried_acc)


def body(
    mamba_x, mamba_b, mamba_c, step_dt, decay_a, skip_d, value_weight, queries, keys, out_grad
):
    tok_rows = mamba_x.shape[0]
    head_count = decay_a.shape[0]
    group_count = mamba_b.shape[1] // STATE
    ctx_count = lax.axis_size("ctx")
    seq_rows = tok_rows * ctx_count
    x_float = mamba_x.astype(jnp.float32).reshape(tok_rows, head_count, HEAD_P)
    b_float = mamba_b.astype(jnp.float32).reshape(tok_rows, group_count, STATE)
    readout_matrix_single = mamba_c.astype(jnp.float32).reshape(tok_rows, group_count, STATE)

    def local_part(arg_x, arg_b, arg_c):
        return block_terms(arg_x, arg_b, arg_c, step_dt, decay_a, skip_d)

    (local_out, end_state, end_decay), pull_local = jax.vjp(
        local_part, x_float, b_float, readout_matrix_single
    )
    identity = (jnp.ones_like(end_decay), jnp.zeros_like(end_state))
    entering = carried_in((end_decay, end_state), "ctx", link_states, identity, False)[1]

    def entry_part(arg_c, arg_entering):
        return entry_terms(arg_c, step_dt, decay_a, arg_entering)

    entry_out, pull_entry = jax.vjp(entry_part, readout_matrix_single, entering)
    mamba_y = (local_out + entry_out).astype(jnp.bfloat16).reshape(tok_rows, head_count * HEAD_P)
    value_terms = jnp.dot(mamba_y, value_weight, preferred_element_type=jnp.float32)
    values = lax.psum_scatter(
        value_terms, ("ch", "section"), scatter_dimension=1, tiled=True
    ).astype(jnp.bfloat16)
    kv_dev = keys.shape[1] // HEAD_DIM
    rep_count = Q_HEADS // KV_HEADS
    query_head_rows = queries.reshape(tok_rows, kv_dev, rep_count, HEAD_DIM)
    gradient_per_head = out_grad.reshape(tok_rows, kv_dev, rep_count, HEAD_DIM)
    key_heads = keys.reshape(tok_rows, kv_dev, HEAD_DIM)
    value_heads = values.reshape(tok_rows, kv_dev, HEAD_DIM)
    own_index = lax.axis_index("ctx")
    query_pos = own_index * tok_rows + jnp.arange(tok_rows)
    scale_by = 1.0 / math.sqrt(HEAD_DIM)

    def masked_scores(key_tile_rows, first_row):
        scores = (
            jnp.einsum(
                "iuan,yun->uaiy", query_head_rows, key_tile_rows, preferred_element_type=jnp.float32
            )
            * scale_by
        )
        visible = (first_row + jnp.arange(key_tile_rows.shape[0]))[None, :] <= query_pos[:, None]
        return (jnp.where(visible, scores, NEG_FILL), visible)

    def add_stats(running, key_tile_rows, value_tile_rows, first_row):
        row_top, row_total = running
        scores, visible = masked_scores(key_tile_rows, first_row)
        new_top = jnp.maximum(row_top, jnp.max(scores, axis=-1))
        block_sum = jnp.sum(jnp.where(visible, jnp.exp(scores - new_top[..., None]), 0.0), axis=-1)
        return (new_top, row_total * jnp.exp(row_top - new_top) + block_sum)

    def probs_of(stats_pair, key_tile_rows, first_row):
        scores, visible = masked_scores(key_tile_rows, first_row)
        return jnp.where(
            visible, jnp.exp(scores - stats_pair[0][..., None]) / stats_pair[1][..., None], 0.0
        )

    def add_output(stats_pair, running, key_tile_rows, value_tile_rows, first_row):
        probability_batch = probs_of(stats_pair, key_tile_rows, first_row).astype(jnp.bfloat16)
        return running + jnp.einsum(
            "vibq,qvu->bviu", probability_batch, value_tile_rows, preferred_element_type=jnp.float32
        )

    def grad_terms(stats_pair, row_delta, key_tile_rows, value_tile_rows, first_row):
        probs = probs_of(stats_pair, key_tile_rows, first_row)
        probability_batch = probs.astype(jnp.bfloat16)
        dprobs = jnp.einsum(
            "iuan,yun->uaiy", gradient_per_head, value_tile_rows, preferred_element_type=jnp.float32
        )
        score_gradient_batch = (probs * (dprobs - row_delta[..., None])).astype(jnp.bfloat16)
        query_term = jnp.einsum(
            "vibq,qvu->bviu",
            score_gradient_batch,
            key_tile_rows,
            preferred_element_type=jnp.float32,
        )
        key_term = (
            jnp.einsum(
                "xucw,cxuh->wxh",
                score_gradient_batch,
                query_head_rows,
                preferred_element_type=jnp.float32,
            )
            * scale_by
        )
        value_term = jnp.einsum(
            "xucw,cxuh->wxh",
            probability_batch,
            gradient_per_head,
            preferred_element_type=jnp.float32,
        )
        return (query_term, key_term, value_term)

    def add_grads(stats_pair, row_delta, running, key_tile_rows, value_tile_rows, first_row):
        query_acc, key_acc, value_acc = running
        query_term, key_term, value_term = grad_terms(
            stats_pair, row_delta, key_tile_rows, value_tile_rows, first_row
        )
        key_acc = lax.dynamic_update_slice_in_dim(key_acc, key_term, first_row, 0)
        value_acc = lax.dynamic_update_slice_in_dim(value_acc, value_term, first_row, 0)
        return (query_acc + query_term, key_acc, value_acc)

    stats_init = (
        jnp.full((kv_dev, rep_count, tok_rows), NEG_FILL, jnp.float32),
        jnp.zeros((kv_dev, rep_count, tok_rows), jnp.float32),
    )
    output_init = jnp.zeros((tok_rows, kv_dev, rep_count, HEAD_DIM), jnp.float32)
    piece = (
        lax.all_gather(key_heads, "ctx", axis=0, tiled=True),
        lax.all_gather(value_heads, "ctx", axis=0, tiled=True),
    )
    stats_pair = blockwise(stats_init, piece[0], piece[1], add_stats)
    piece = (
        lax.all_gather(key_heads, "ctx", axis=0, tiled=True),
        lax.all_gather(value_heads, "ctx", axis=0, tiled=True),
    )
    output_acc = blockwise(
        output_init, piece[0], piece[1], functools.partial(add_output, stats_pair)
    )
    delta_rows = jnp.sum(gradient_per_head.astype(jnp.float32) * output_acc, axis=-1)
    row_delta = delta_rows.transpose(1, 2, 0)
    grads_init = (
        jnp.zeros((tok_rows, kv_dev, rep_count, HEAD_DIM), jnp.float32),
        jnp.zeros((seq_rows, kv_dev, HEAD_DIM), jnp.float32),
        jnp.zeros((seq_rows, kv_dev, HEAD_DIM), jnp.float32),
    )
    piece = (
        lax.all_gather(key_heads, "ctx", axis=0, tiled=True),
        lax.all_gather(value_heads, "ctx", axis=0, tiled=True),
    )
    query_acc, key_acc, value_acc = blockwise(
        grads_init, piece[0], piece[1], functools.partial(add_grads, stats_pair, row_delta)
    )
    key_local, value_local = (
        lax.psum_scatter(key_acc, "ctx", scatter_dimension=0, tiled=True),
        lax.psum_scatter(value_acc, "ctx", scatter_dimension=0, tiled=True),
    )
    attn_out = output_acc.reshape(tok_rows, kv_dev * rep_count * HEAD_DIM)
    grad_q = (query_acc * scale_by).reshape(tok_rows, kv_dev * rep_count * HEAD_DIM)
    grad_k = key_local.reshape(tok_rows, kv_dev * HEAD_DIM)
    value_grad = value_local.astype(jnp.bfloat16).reshape(tok_rows, kv_dev * HEAD_DIM)
    mamba_grad = lax.dot_general(
        lax.all_gather(value_grad, ("ch", "section"), axis=1, tiled=True),
        value_weight,
        (((1,), (1,)), ((), ())),
        preferred_element_type=jnp.float32,
    )
    grad_heads_y = mamba_grad.reshape(tok_rows, head_count, HEAD_P)
    c_entry_grad, entering_grad = pull_entry(grad_heads_y)
    state_grad = carried_in((end_decay, entering_grad), "ctx", link_states, identity, True)[1]
    x_grad, b_grad, c_local_grad = pull_local((grad_heads_y, state_grad, jnp.zeros_like(end_decay)))
    grad_x = x_grad.reshape(tok_rows, head_count * HEAD_P)
    grad_b = b_grad.reshape(tok_rows, group_count * STATE)
    grad_c = (c_local_grad + c_entry_grad).reshape(tok_rows, group_count * STATE)
    return (attn_out, grad_q, grad_k, grad_x, grad_b, grad_c)


def solution(mesh):
    in_specs = (
        P("ctx", ("ch", "section")),
        P("ctx", ("ch", "section")),
        P("ctx", ("ch", "section")),
        P("ctx", ("ch", "section")),
        P(("ch", "section")),
        P(("ch", "section")),
        P(("ch", "section"), None),
        P("ctx", ("ch", "section")),
        P("ctx", ("ch", "section")),
        P("ctx", ("ch", "section")),
    )
    out_specs = (
        P("ctx", ("ch", "section")),
        P("ctx", ("ch", "section")),
        P("ctx", ("ch", "section")),
        P("ctx", ("ch", "section")),
        P("ctx", ("ch", "section")),
        P("ctx", ("ch", "section")),
    )
    return jax.shard_map(body, mesh=mesh, in_specs=in_specs, out_specs=out_specs, check_vma=False)
```

profile of v0, /device:TPU:0, one launch (start us, length us, event | category | flops | bytes accessed | tf_op | source)
XLA Modules:
  0.0 1288.6 jit_solution(10932054022057228586)
XLA Ops:
  16.6 95.5 %all-gather.2 = f32[32,1,16]{2,1,0:T(1,128)S(1)} all-gather(f32[1,1,16]{2,1,0:T(1,128)S(1)} %get-tuple-element.843), channel_id=1, replica_groups=mesh['ctx'=32,'ch'=2,'section'=2] {'ctx'}, dimensions={0}, use_global_device_ids=true | all-gather | bytes 2112 | tf_op jit(solution)/shard_map/all_gather | solution.py:24
  113.4 165.5 %all-gather.12.cloned.1.call-done = f32[512,128,128]{2,1,0:T(8,128)} async-done(((f32[16,128,128]{2,1,0:T(8,128)}), f32[512,128,128]{2,1,0:T(8,128)}) %all-gather.12.cloned.1.call-update) | async-done | bytes 33554448 | tf_op jit(solution)/shard_map/all_gather | solution.py:24
  287.1 70.2 %all-gather.10.cloned.1.call-done = bf16[4096,2,128]{0,2,1:T(8,128)(2,1)} async-done(((bf16[128,2,128]{0,2,1:T(8,128)(2,1)}), bf16[4096,2,128]{0,2,1:T(8,128)(2,1)}) %all-gather.10.cloned.1.call-update) | async-done | bytes 2097168 | tf_op jit(solution)/shard_map/all_gather | solution.py:202
  357.3 4.1 copy.108
  361.4 15.7 %reduce-scatter.4.cloned.1.call-done = f32[128,256]{1,0:T(8,128)} async-done(((f32[128,1024]{1,0:T(8,128)}), f32[128,256]{1,0:T(8,128)}) %reduce-scatter.4.cloned.1.call-update) | async-done | bytes 131088 | tf_op jit(solution)/shard_map/reduce_scatter | solution.py:110
  378.8 56.4 %while.76 = (s32[]{:T(128)}, f32[2,8,128]{2,1,0:T(8,128)S(1)}, f32[2,8,128]{2,1,0:T(8,128)S(1)}, bf16[4096,2,128]{2,0,1:T(8,128)(2,1)}, bf16[128,2,8,128]{3,0,2,...) while((s32[]{:T(128)}, f32[2,8,128]{2,1,0:T(8,128)S(1)}, ...), condition=%wide.region_7.8_spmd.clone, body=%wide.region_4.7_spmd.clone.sunk | while | flops 276900480 | bytes 9483442 | solution.py:80
  379.0 3.6 fusion.140
  382.7 3.2 select_reduce_fusion.2
  386.1 3.6 fusion.140
  389.7 3.2 select_reduce_fusion.2
  393.1 3.6 fusion.140
  396.7 3.2 select_reduce_fusion.2
  400.2 3.6 fusion.140
  403.8 3.2 select_reduce_fusion.2
  407.2 3.6 fusion.140
  410.8 3.3 select_reduce_fusion.2
  414.3 3.6 fusion.140
  417.9 3.2 select_reduce_fusion.2
  421.3 3.6 fusion.140
  425.0 3.2 select_reduce_fusion.2
  428.4 3.6 fusion.140
  432.0 3.2 select_reduce_fusion.2
  435.3 18.5 %all-gather.8.cloned.1.call-done = bf16[4096,2,128]{2,0,1:T(8,128)(2,1)} async-done(((bf16[128,2,128]{2,0,1:T(8,128)(2,1)}), bf16[4096,2,128]{2,0,1:T(8,128)(2,1)}) %all-gather.8.cloned.1.call-update) | async-done | bytes 2097168 | tf_op jit(solution)/shard_map/all_gather | solution.py:203
  453.8 23.3 %while.77 = (s32[]{:T(128)}, f32[128,2,8,128]{0,3,2,1:T(8,128)S(1)}, bf16[4096,2,128]{2,0,1:T(8,128)(2,1)}, bf16[4096,2,128]{2,0,1:T(8,128)(2,1)}, bf16[128,2,8,...) while((s32[]{:T(128)}, ...), condition=%wide.region_9.10_spmd.clone, body=%wide.region_8.9_spmd.clone.sunk | while | flops 543752832 | bytes 3300028 | solution.py:80
  482.0 107.6 %while.78 = (s32[]{:T(128)}, f32[128,2,8,128]{0,3,2,1:T(8,128)}, f32[4096,2,128]{2,0,1:T(8,128)}, f32[4096,2,128]{0,2,1:T(8,128)}, bf16[4096,2,128]{2,0,1:T(8,12...) while((s32[]{:T(128)}, f32[128,2,8,128]{0,3,2,1:T(8,128)}, ...), condition=%wide.region_12.13_spmd.clone, body=%wide.region_11.12_spmd.clone.sunk | while | flops 1352336000 | bytes 69105048 | solution.py:80
  590.2 188.6 %reduce-scatter.8.cloned.1.call-done = f32[128,2,128]{0,2,1:T(8,128)} async-done(((f32[4096,2,128]{0,2,1:T(8,128)}), f32[128,2,128]{0,2,1:T(8,128)}) %reduce-scatter.8.cloned.1.call-update) | async-done | bytes 131088 | tf_op jit(solution)/shard_map/reduce_scatter | solution.py:224
  779.7 6.0 all_gather.35
  785.7 3.4 fusion.83
  789.2 3.5 fusion.69
  803.1 165.2 %reduce-scatter.6.cloned.1.call-done = f32[128,2,128]{2,0,1:T(8,128)} async-done(((f32[4096,2,128]{2,0,1:T(8,128)}), f32[128,2,128]{2,0,1:T(8,128)}) %reduce-scatter.6.cloned.1.call-update) | async-done | bytes 131088 | tf_op jit(solution)/shard_map/reduce_scatter | solution.py:223
  969.8 257.8 %all-gather.14.cloned.1.call-done = f32[512,128,128]{2,1,0:T(8,128)} async-done(((f32[16,128,128]{2,1,0:T(8,128)}), f32[512,128,128]{2,1,0:T(8,128)}) %all-gather.14.cloned.1.call-update) | async-done | bytes 33554448 | tf_op jit(solution)/shard_map/all_gather | solution.py:24
  1227.7 46.4 %while.75 = (s32[]{:T(128)}, f32[16,128,128]{2,1,0:T(8,128)S(1)}, s32[]{:T(128)}, f32[32,16]{1,0:T(8,128)S(1)}, f32[32,16,128,128]{3,2,1,0:T(8,128)}, /*index=5*/s32[]{:T(128)}, s32[]{:T(128)}, s32[]{:T(128)}, s32[]{:T(128)}) while((s32[]{:T(128)}, f32[16,128,128]{2,1,0:T(8,128)S(1)}, s32[]{:T(128)}, f32[32,16]{1,0:T(8,128)S(1)}, ...), condition=%wide.region_16.17_spmd, body=%wide.region_15.16_spmd.sunk | while | flops 524294 | bytes 3146075 | solution.py:33
  (421 shorter events, 222.7 us)
Async XLA Ops:
  7.2 9.1 copy-start.18
  7.2 7.6 copy-start.19
  7.2 8.5 copy-start.20
  7.2 271.8 %all-gather.12.cloned.1.call-start = ((), (), s32[]{:S(2)}) async-start(), calls=%async_computation.8 | async-start | bytes 34603008 | tf_op jit(solution)/shard_map/all_gather | solution.py:24
  11.1 102.3 %copy-start.13 = (bf16[128,2048]{0,1:T(8,128)(2,1)}, bf16[128,2048]{0,1:T(8,128)(2,1)S(1)}, u32[]{:S(2)}) copy-start(bf16[128,2048]{0,1:T(8,128)(2,1)S(1)} %copy.96) | copy-start | bytes 1572868
  11.1 101.1 %copy-start.21 = (f32[16]{0:T(128)S(1)}, f32[16]{0:T(128)}, u32[]{:S(2)}) copy-start(f32[16]{0:T(128)} %param.25) | copy-start | bytes 196
  14.7 342.6 %all-gather.10.cloned.1.call-start = ((), (), s32[]{:S(2)}) async-start(), calls=%async_computation.5 | async-start | bytes 2162688 | tf_op jit(solution)/shard_map/all_gather | solution.py:202
  15.5 361.5 %reduce-scatter.4.cloned.1.call-start = ((), (), s32[]{:S(2)}) async-start(), calls=%async_computation.3 | async-start | bytes 655360 | tf_op jit(solution)/shard_map/reduce_scatter | solution.py:110
  16.6 95.6 %copy-start.11 = (f32[16,128,128]{2,1,0:T(8,128)}, f32[16,128,128]{2,1,0:T(8,128)S(1)}, u32[]{:S(2)}) copy-start(f32[16,128,128]{2,1,0:T(8,128)S(1)} %fusion.71) | copy-start | bytes 3145732
  284.1 169.7 %all-gather.8.cloned.1.call-start = ((), (), s32[]{:S(2)}) async-start(), calls=%async_computation.4 | async-start | bytes 2162688 | tf_op jit(solution)/shard_map/all_gather | solution.py:203
  378.6 400.2 %reduce-scatter.8.cloned.1.call-start = ((), (), s32[]{:S(2)}) async-start(), calls=%async_computation.7 | async-start | bytes 4325376 | tf_op jit(solution)/shard_map/reduce_scatter | solution.py:224
  477.1 4.9 copy-start.16
  488.2 5.2 copy-start.1
  488.2 5.2 copy-start.3
  501.3 5.5 copy-start.1
  501.4 5.5 copy-start.3
  514.8 5.5 copy-start.1
  514.8 5.5 copy-start.3
  528.3 5.5 copy-start.1
  528.3 5.5 copy-start.3
  541.8 5.5 copy-start.1
  541.8 5.5 copy-start.3
  555.3 5.5 copy-start.1
  555.3 5.5 copy-start.3
  568.8 5.5 copy-start.1
  568.8 5.5 copy-start.3
  582.3 5.5 copy-start.1
  582.3 5.5 copy-start.3
  589.6 378.6 %reduce-scatter.6.cloned.1.call-start = ((), (), s32[]{:S(2)}) async-start(), calls=%async_computation.6 | async-start | bytes 4325376 | tf_op jit(solution)/shard_map/reduce_scatter | solution.py:223
  590.2 637.4 %all-gather.14.cloned.1.call-start = ((), (), s32[]{:S(2)}) async-start(), calls=%async_computation.9 | async-start | bytes 34603008 | tf_op jit(solution)/shard_map/all_gather | solution.py:24
  789.2 6.0 copy-start.6
  1227.7 46.4 %copy-start.10 = (f32[128,2,8,128]{3,0,2,1:T(8,128)S(1)}, f32[128,2,8,128]{3,0,2,1:T(8,128)}, u32[]{:S(2)}) copy-start(f32[128,2,8,128]{3,0,2,1:T(8,128)} %copy-done.9) | copy-start | bytes 3145732
  (39 other events, 103.0 us)
Sparse Core Ops, SparseCore 0:
  14.8 264.0 all-gather.11
  282.3 74.9 all-gather.9
  360.3 16.7 reduce-scatter.3
  380.6 73.1 all-gather.7
  589.7 189.0 reduce-scatter.7
  781.1 187.1 reduce-scatter.5
  971.4 256.2 all-gather.13
where the time goes:
time: 1290 us
  waiting for transfers between devices  882 us (68%)
  matrix products  155 us (12%)
  blocking collectives  102 us (8%)
  other arithmetic  79.1 us (6%)
  local copies, waits for them, and re-layouts  53.1 us (4%)
  between operations  14.6 us (1%)
    all_gather x2, waiting for transfers between devices, carried_in(): gathered = jax.tree.map(lambda a: lax.all_gather(a, axis), part)  423 us
    reduce_scatter x1, waiting for transfers between devices, body(): lax.psum_scatter(value_acc, 'ctx', scatter_dimension=0, tiled=True)  189 us
    reduce_scatter x1, waiting for transfers between devices, body(): lax.psum_scatter(key_acc, 'ctx', scatter_dimension=0, tiled=True)  165 us
    all_gather x1, blocking collectives, carried_in(): gathered = jax.tree.map(lambda a: lax.all_gather(a, axis), part)  95.5 us
    all_gather x1, waiting for transfers between devices, body(): lax.all_gather(key_heads, 'ctx', axis=0, tiled=True)  70.2 us
    dot_general x16, matrix products, masked_scores(): jnp.einsum('iuan,yun->uaiy', query_head_rows, key_tile_rows, preferred_el...  47.4 us
    add x31, other arithmetic, link_states(): later[0][:, None, None] * earlier[1] + later[1]  44.9 us
  transfers between devices with their start and end apart: 7, of which 7 were waited for; matrix products, arithmetic and copies ran while one was open for 7% of the time, Pallas kernels for 0%

commit v1 on v0

v1 whole, which is shorter than its diff:
```python
import math

import jax
import jax.numpy as jnp
from jax import lax
from jax.experimental import pallas as pl
from jax.experimental.pallas import tpu as pltpu
from jax.sharding import PartitionSpec as P

T = 128
NH = 16
GH = 8
F32 = jnp.float32
BF = jnp.bfloat16
HI = lax.Precision.HIGHEST
SCALE = 1.0 / math.sqrt(128.0)
SR = 64
DR = 16
NEG = -1e30

NN = (((1,), (0,)), ((), ()))
NT = (((1,), (1,)), ((), ()))
TN = (((0,), (0,)), ((), ()))


def mm(a, b, dims=NN):
    return lax.dot_general(a, b, dims, preferred_element_type=F32)


def mm_exact(a, b, dims=NN):
    return lax.dot_general(a, b, dims, precision=HI, preferred_element_type=F32)


def head(h):
    return slice(h * T, (h + 1) * T)


def lower_tri():
    row = lax.broadcasted_iota(jnp.int32, (T, T), 0)
    col = lax.broadcasted_iota(jnp.int32, (T, T), 1)
    return row >= col


def sums_by_token(dt_ref, a_ref):
    steps = -dt_ref[...] * a_ref[...]
    return mm_exact(lower_tri().astype(F32), steps)


def sums_by_head(dt_ref, a_ref):
    row = lax.broadcasted_iota(jnp.int32, (T, T), 0)
    col = lax.broadcasted_iota(jnp.int32, (T, T), 1)
    steps = -dt_ref[...] * a_ref[...]
    upper = (row <= col).astype(F32)
    same = (row == col).astype(F32)
    return mm_exact(steps, upper, TN), mm_exact(dt_ref[...], same, TN)


def state_kernel(x_ref, b_ref, dt_ref, a_ref, k_ref, out_ref):
    cum = sums_by_token(dt_ref, a_ref)
    total = cum[T - 1 : T, :]
    weight = jnp.exp(total - cum) * dt_ref[...]
    first = total.astype(BF).astype(F32)
    second = (total - first).astype(BF).astype(F32)
    third = total - first - second
    row = lax.broadcasted_iota(jnp.int32, (DR, T), 0)
    for h in range(NH):
        g = h // GH
        xw = (x_ref[:, head(h)].astype(F32) * weight[:, h : h + 1]).astype(BF)
        state = mm(xw, b_ref[:, head(g)], TN).astype(BF)
        parts = jnp.where(
            row == 0,
            first[:, h : h + 1],
            jnp.where(row == 1, second[:, h : h + 1], third[:, h : h + 1]),
        ).astype(BF)
        for half in range(2):
            d = 2 * h + half
            out_ref[d, 0:SR, :] = state[half * SR : (half + 1) * SR]
            out_ref[d, SR : SR + DR, :] = parts
    for d in range(32):
        out_ref[d, SR + DR : SR + DR + T, :] = k_ref[:, head(d // 16)]


def decay_of(r1_ref, c):
    parts = r1_ref[c, SR : SR + DR, :].astype(F32)
    return jnp.exp(parts[0:1] + parts[1:2] + parts[2:3])


def probs_kernel(
    at_ref, r1_ref, q_ref, d_ref, other_ref, pay_ref, p_ref, qs_ref, ds_ref, s_sc, dv_sc
):
    at = at_ref[0]
    upper = (at >= 16).astype(jnp.int32)
    low = jnp.minimum(at, 31 - at)

    run = jnp.zeros((SR, T), F32)
    for c in range(32):
        pay_ref[c, 0:SR, :] = run.astype(BF)
        run = decay_of(r1_ref, c) * run + r1_ref[c, 0:SR, :].astype(F32)

    for h in range(GH):
        own = pl.ds(pl.multiple_of(upper * 1024 + h * T, T), T)
        qs_ref[upper, head(h), :] = q_ref[:, own]
        ds_ref[upper, head(h), :] = d_ref[:, own]
        qs_ref[1 - upper, head(h), :] = other_ref[0:T, head(h)]
        ds_ref[1 - upper, head(h), :] = other_ref[T : 2 * T, head(h)]

    dv_sc[...] = jnp.zeros_like(dv_sc)
    key = lax.broadcasted_iota(jnp.int32, (T, 256), 0)
    tok = lax.broadcasted_iota(jnp.int32, (T, 256), 1) & (T - 1)
    seen = key <= tok

    for sel in range(2):
        count = low if sel == 0 else 31 - low
        base = 0 if sel == 0 else low + 1

        def scores(j, top, diag, sel=sel, base=base):
            k = r1_ref[j, SR + DR : SR + DR + T, :]
            tops = []
            for c in range(4):
                cols = slice(c * 256, (c + 1) * 256)
                s = mm(k, qs_ref[sel, cols, :], NT)
                if diag:
                    s = jnp.where(seen, s, NEG)
                s_sc[base + j, :, cols] = s
                tops.append(jnp.maximum(top[c], jnp.max(s.reshape(16, 8, 256), axis=0)))
            return tuple(tops)

        top = tuple(jnp.full((8, 256), NEG, F32) for _ in range(4))
        top = lax.fori_loop(0, count, lambda j, t: scores(j, t, False), top)
        top = scores(count, top, True)
        peak = [jnp.max(t, axis=0, keepdims=True) for t in top]

        def weigh(j, tot, base=base, peak=peak):
            tots = []
            for c in range(4):
                cols = slice(c * 256, (c + 1) * 256)
                p = jnp.exp((s_sc[base + j, :, cols] - peak[c]) * SCALE)
                s_sc[base + j, :, cols] = p
                tots.append(tot[c] + jnp.sum(p.reshape(16, 8, 256), axis=0))
            return tuple(tots)

        tot = tuple(jnp.zeros((8, 256), F32) for _ in range(4))
        tot = lax.fori_loop(0, count + 1, weigh, tot)
        inv = [1.0 / jnp.sum(t, axis=0, keepdims=True) for t in tot]

        def spread(j, none, sel=sel, base=base, inv=inv):
            acc = dv_sc[j]
            for c in range(4):
                cols = slice(c * 256, (c + 1) * 256)
                p = (s_sc[base + j, :, cols] * inv[c]).astype(BF)
                p_ref[base + j, :, cols] = p
                acc = acc + mm(p, ds_ref[sel, cols, :])
            dv_sc[j] = acc
            return none

        lax.fori_loop(0, count + 1, spread, 0)

    for c in range(32):
        pay_ref[c, SR : SR + T, :] = dv_sc[c].astype(BF)


def values_kernel(
    x_ref, b_ref, c_ref, dt_ref, a_ref, skip_ref, r2_ref, w_ref, out_ref, y_sc
):
    cum = sums_by_token(dt_ref, a_ref)
    cum_t, dt_t = sums_by_head(dt_ref, a_ref)
    grow = jnp.exp(cum)
    lower = lower_tri()
    for g in range(2):
        cb = mm(c_ref[:, head(g)], b_ref[:, head(g)], NT)
        for h in range(g * GH, (g + 1) * GH):
            gap = cum[:, h : h + 1] - cum_t[h : h + 1, :]
            mix = cb * jnp.exp(jnp.where(lower, gap, NEG)) * dt_t[h : h + 1, :]
            x = x_ref[:, head(h)]
            enter = jnp.concatenate([r2_ref[2 * h, 0:SR, :], r2_ref[2 * h + 1, 0:SR, :]], 0)
            y = mm(mix.astype(BF), x) + skip_ref[:, h : h + 1] * x.astype(F32)
            y = y + grow[:, h : h + 1] * mm(c_ref[:, head(g)], enter, NT)
            y_sc[:, head(h)] = y.astype(BF)
    dv = []
    for k in range(2):
        acc = r2_ref[16 * k, SR : SR + T, :].astype(F32)
        for s in range(1, 16):
            acc = acc + r2_ref[16 * k + s, SR : SR + T, :].astype(F32)
        dv.append(acc.astype(BF))
    for d in range(4):
        cols = slice(d * 256, (d + 1) * 256)
        out_ref[d, :, 0:256] = mm(y_sc[...], w_ref[:, cols]).astype(BF)
        out_ref[d, :, 256:384] = dv[0]
        out_ref[d, :, 384:512] = dv[1]


def back_kernel(r3_ref, w_ref, c_ref, dt_ref, a_ref, pay_ref, dy_ref):
    values = r3_ref[0, :, 0:256].astype(F32)
    for s in range(1, 4):
        values = values + r3_ref[s, :, 0:256].astype(F32)
    values = values.astype(BF)
    for d in range(32):
        pay_ref[d, SR : SR + T, :] = values[:, head(d // 16)]
    vg = jnp.concatenate([r3_ref[s, :, 256:512] for s in range(4)], axis=1)
    grow = jnp.exp(sums_by_token(dt_ref, a_ref))
    for h in range(NH):
        dy = mm(vg, w_ref[head(h), :], NT)
        dy_ref[:, head(h)] = dy
        eg = mm((dy * grow[:, h : h + 1]).astype(BF), c_ref[:, head(h // GH)], TN).astype(BF)
        pay_ref[2 * h, 0:SR, :] = eg[0:SR]
        pay_ref[2 * h + 1, 0:SR, :] = eg[SR:T]


def grads_kernel(
    at_ref, r1_ref, r4_ref, p_ref, qs_ref, ds_ref, pay_ref, o_ref, send_ref,
    dp_sc, o_sc, dq_sc, dk_sc
):
    at = at_ref[0]
    upper = (at >= 16).astype(jnp.int32)
    low = jnp.minimum(at, 31 - at)

    run = jnp.zeros((SR, T), F32)
    for c in range(31, -1, -1):
        pay_ref[c, 0:SR, :] = run.astype(BF)
        run = decay_of(r1_ref, c) * run + r4_ref[c, 0:SR, :].astype(F32)

    dk_sc[...] = jnp.zeros_like(dk_sc)
    o_sc[...] = jnp.zeros_like(o_sc)
    dq_sc[...] = jnp.zeros_like(dq_sc)
    for sel in range(2):
        count = low if sel == 0 else 31 - low
        base = 0 if sel == 0 else low + 1

        def first(j, delta, sel=sel, base=base):
            v = r4_ref[j, SR : SR + T, :]
            deltas = []
            for c in range(4):
                cols = slice(c * 256, (c + 1) * 256)
                p = p_ref[base + j, :, cols]
                dp = mm(v, ds_ref[sel, cols, :], NT)
                dp_sc[base + j, :, cols] = dp
                term = p.astype(F32) * dp
                deltas.append(delta[c] + jnp.sum(term.reshape(16, 8, 256), axis=0))
                o_sc[sel, :, cols] += mm(v, p, TN)
            return tuple(deltas)

        delta = tuple(jnp.zeros((8, 256), F32) for _ in range(4))
        delta = lax.fori_loop(0, count + 1, first, delta)
        delta = [jnp.sum(t, axis=0, keepdims=True) for t in delta]

        def second(j, none, sel=sel, base=base, delta=delta):
            k = r1_ref[j, SR + DR : SR + DR + T, :]
            acc = dk_sc[j]
            for c in range(4):
                cols = slice(c * 256, (c + 1) * 256)
                p = p_ref[base + j, :, cols].astype(F32)
                ds = (p * (dp_sc[base + j, :, cols] - delta[c])).astype(BF)
                dq_sc[sel, :, cols] += mm(k, ds, TN)
                acc = acc + mm(ds, qs_ref[sel, cols, :])
            dk_sc[j] = acc
            return none

        lax.fori_loop(0, count + 1, second, 0)

    for c in range(32):
        pay_ref[c, SR : SR + T, :] = dk_sc[c].astype(BF)
    for h in range(GH):
        o_ref[0:T, head(h)] = jnp.transpose(o_sc[upper, :, head(h)])
        o_ref[T : 2 * T, head(h)] = jnp.transpose(dq_sc[upper, :, head(h)]) * SCALE
        send_ref[0:T, head(h)] = jnp.transpose(o_sc[1 - upper, :, head(h)]).astype(BF)
        send_ref[T : 2 * T, head(h)] = (
            jnp.transpose(dq_sc[1 - upper, :, head(h)]) * SCALE
        ).astype(BF)


def final_kernel(
    x_ref, b_ref, c_ref, dt_ref, a_ref, skip_ref, dy_ref, r2_ref, r5_ref,
    gx_ref, gb_ref, gc_ref, gk_ref
):
    cum = sums_by_token(dt_ref, a_ref)
    cum_t, dt_t = sums_by_head(dt_ref, a_ref)
    grow = jnp.exp(cum)
    weight = jnp.exp(cum[T - 1 : T, :] - cum) * dt_ref[...]
    lower = lower_tri()
    for g in range(2):
        b = b_ref[:, head(g)]
        cc = c_ref[:, head(g)]
        cb = mm(cc, b, NT)
        mixed = jnp.zeros((T, T), F32)
        gb = jnp.zeros((T, T), F32)
        gc = jnp.zeros((T, T), F32)
        for h in range(g * GH, (g + 1) * GH):
            gap = cum[:, h : h + 1] - cum_t[h : h + 1, :]
            decay = jnp.exp(jnp.where(lower, gap, NEG)) * dt_t[h : h + 1, :]
            mix = (cb * decay).astype(BF)
            x = x_ref[:, head(h)]
            dy = dy_ref[:, head(h)]
            dyb = dy.astype(BF)
            enter = jnp.concatenate([r2_ref[2 * h, 0:SR, :], r2_ref[2 * h + 1, 0:SR, :]], 0)
            sg = jnp.concatenate([r5_ref[2 * h, 0:SR, :], r5_ref[2 * h + 1, 0:SR, :]], 0)
            gx = mm(mix, dyb, TN) + skip_ref[:, h : h + 1] * dy
            gx_ref[:, head(h)] = gx + weight[:, h : h + 1] * mm(b, sg, NT)
            mixed = mixed + mm(dyb, x, NT) * decay
            gb = gb + weight[:, h : h + 1] * mm(x, sg)
            gc = gc + grow[:, h : h + 1] * mm(dyb, enter)
        mixed = mixed.astype(BF)
        gb_ref[:, head(g)] = gb + mm(mixed, cc, TN)
        gc_ref[:, head(g)] = gc + mm(mixed, b)
    for k in range(2):
        acc = r5_ref[16 * k, SR : SR + T, :].astype(F32)
        for s in range(1, 16):
            acc = acc + r5_ref[16 * k + s, SR : SR + T, :].astype(F32)
        gk_ref[:, head(k)] = acc * SCALE


VM = pl.BlockSpec(memory_space=pltpu.VMEM)
SM = pl.BlockSpec(memory_space=pltpu.SMEM)


def call(kernel, outs, scratch, name, mib, flops, nbytes, *args):
    return pl.pallas_call(
        kernel,
        name=name,
        out_shape=[jax.ShapeDtypeStruct(s, d) for s, d in outs],
        in_specs=[SM if a.dtype == jnp.int32 else VM for a in args],
        out_specs=[VM] * len(outs),
        scratch_shapes=[pltpu.VMEM(s, d) for s, d in scratch],
        cost_estimate=pl.CostEstimate(
            flops=flops, bytes_accessed=nbytes, transcendentals=0
        ),
        compiler_params=pltpu.CompilerParams(vmem_limit_bytes=mib << 20),
    )(*args)


def over_ctx(pay):
    return lax.all_to_all(pay, "ctx", 0, 0, tiled=True)


def body(
    mamba_x, mamba_b, mamba_c, step_dt, decay_a, skip_d, value_weight, queries, keys, out_grad
):
    at = lax.axis_index("ctx")
    at1 = at.astype(jnp.int32).reshape(1)
    upper = at >= 16
    a_row = decay_a.reshape(1, NH)
    skip_row = skip_d.reshape(1, NH)
    swap = [(i, 31 - i) for i in range(32)]

    away = jnp.concatenate(
        [
            jnp.where(upper, queries[:, :1024], queries[:, 1024:]),
            jnp.where(upper, out_grad[:, :1024], out_grad[:, 1024:]),
        ],
        axis=0,
    )
    other = lax.ppermute(away, "ctx", swap)
    (pay1,) = call(
        state_kernel, [((32, SR + DR + T, T), BF)], [], "block_states", 24, 1 << 27, 1 << 22,
        mamba_x, mamba_b, step_dt, a_row, keys,
    )
    r1 = over_ctx(pay1)
    pay2, probs, qs, ds = call(
        probs_kernel,
        [((32, SR + T, T), BF), ((33, T, 1024), BF), ((2, 1024, T), BF), ((2, 1024, T), BF)],
        [((33, T, 1024), F32), ((32, T, T), F32)],
        "probs", 56, 1 << 32, 1 << 24, at1, r1, queries, out_grad, other,
    )
    r2 = over_ctx(pay2)
    (pay3,) = call(
        values_kernel, [((4, T, 512), BF)], [((T, 2048), BF)], "values", 32, 1 << 30, 1 << 23,
        mamba_x, mamba_b, mamba_c, step_dt, a_row, skip_row, r2, value_weight,
    )
    r3 = lax.all_to_all(pay3, ("ch", "section"), 0, 0, tiled=True)
    pay4, dy = call(
        back_kernel, [((32, SR + T, T), BF), ((T, 2048), F32)], [], "value_back", 32, 1 << 30,
        1 << 23, r3, value_weight, mamba_c, step_dt, a_row,
    )
    r4 = over_ctx(pay4)
    pay5, kept, send = call(
        grads_kernel,
        [((32, SR + T, T), BF), ((256, 1024), F32), ((256, 1024), BF)],
        [((33, T, 1024), F32), ((2, T, 1024), F32), ((2, T, 1024), F32), ((32, T, T), F32)],
        "attention_grads", 60, 1 << 32, 1 << 24, at1, r1, r4, probs, qs, ds,
    )
    back = lax.ppermute(send, "ctx", swap)
    r5 = over_ctx(pay5)
    grad_x, grad_b, grad_c, grad_k = call(
        final_kernel,
        [((T, 2048), F32), ((T, 256), F32), ((T, 256), F32), ((T, 256), F32)],
        [], "mixer_grads", 32, 1 << 29, 1 << 23,
        mamba_x, mamba_b, mamba_c, step_dt, a_row, skip_row, dy, r2, r5,
    )
    back = back.astype(F32)
    whole = jnp.where(
        upper, jnp.concatenate([back, kept], axis=1), jnp.concatenate([kept, back], axis=1)
    )
    return (whole[:T], whole[T:], grad_k, grad_x, grad_b, grad_c)


def solution(mesh):
    tokens = P("ctx", ("ch", "section"))
    heads = P(("ch", "section"))
    in_specs = (
        tokens, tokens, tokens, tokens, heads, heads, P(("ch", "section"), None),
        tokens, tokens, tokens,
    )
    return jax.shard_map(
        body, mesh=mesh, in_specs=in_specs, out_specs=(tokens,) * 6, check_vma=False
    )
```

time: 1290 us -> 233 us (0.18)
  waiting for transfers between devices: 882 us -> 56.6 us
  matrix products: 155 us -> 0 us
  other arithmetic: 79.1 us -> 0.54 us
  Pallas kernels: 0 us -> 66.8 us
  local copies, waits for them, and re-layouts: 53.1 us -> 9.31 us
  blocking collectives: 102 us -> 68.1 us
  starting transfers between devices: 0.46 us -> 30.4 us
  between operations: 14.6 us -> 0.82 us
    all_gather x4 -> x0, waiting for transfers between devices: 512 us -> none  [the longest x2 423 us: carried_in(): gathered = jax.tree.map(lambda a: lax.all_gather(a, axis), part)]
    reduce_scatter x3 -> x0, waiting for transfers between devices: 369 us -> none  [the longest x1 189 us: body(): lax.psum_scatter(value_acc, 'ctx', scatter_dimension=0, tiled=True)]
    dot_general x70 -> x0, matrix products: 155 us -> none  [the longest x16 47.4 us: masked_scores(): jnp.einsum('iuan,yun->uaiy', query_head_rows, key_tile_rows, preferred_el...]
    all_gather x2 -> x0, blocking collectives: 102 us -> none  [the longest x1 95.5 us: carried_in(): gathered = jax.tree.map(lambda a: lax.all_gather(a, axis), part)]
    all_to_all x0 -> x3, blocking collectives: none -> 68.1 us  [the longest x2 56.9 us: over_ctx(): return lax.all_to_all(pay, 'ctx', 0, 0, tiled=True)]
    pallas_call x0 -> x6, Pallas kernels: none -> 66.8 us  [call(): pl.pallas_call(kernel, name=name, out_shape=[jax.ShapeDtypeStruct(s, d) f...]
    ppermute x0 -> x2, waiting for transfers between devices: none -> 56.6 us  [the longest x1 29.5 us: body(): other = lax.ppermute(away, 'ctx', swap)]
    add x87 -> x0, other arithmetic: 45.2 us -> none  [the longest x31 44.9 us: link_states(): later[0][:, None, None] * earlier[1] + later[1]]
  transfers between devices with their start and end apart: 7 -> 4, of which waited for: 7 -> 2; matrix products, arithmetic and copies ran while one was open for 7% -> 1% of each run, Pallas kernels for 0% -> 0%
where the time goes in v1:
time: 233 us
  blocking collectives  68.1 us (29%)
  Pallas kernels  66.8 us (29%)
  waiting for transfers between devices  56.6 us (24%)
  starting transfers between devices  30.4 us (13%)
  local copies, waits for them, and re-layouts  9.31 us (4%)
    pallas_call x6, Pallas kernels, call(): pl.pallas_call(kernel, name=name, out_shape=[jax.ShapeDtypeStruct(s, d) f...  66.8 us
    all_to_all x2, blocking collectives, over_ctx(): return lax.all_to_all(pay, 'ctx', 0, 0, tiled=True)  56.9 us
    ppermute x1, waiting for transfers between devices, body(): other = lax.ppermute(away, 'ctx', swap)  29.5 us
    ppermute x1, waiting for transfers between devices, body(): back = lax.ppermute(send, 'ctx', swap)  27.1 us
    all_to_all x2, starting transfers between devices, over_ctx(): return lax.all_to_all(pay, 'ctx', 0, 0, tiled=True)  14.8 us
    all_to_all x1, blocking collectives, body(): r3 = lax.all_to_all(pay3, ('ch', 'section'), 0, 0, tiled=True)  11.2 us
    ppermute x1, starting transfers between devices, body(): back = lax.ppermute(send, 'ctx', swap)  7.87 us
    unnamed x37, local copies, waits for them, and re-layouts  7.85 us
  transfers between devices with their start and end apart: 4, of which 2 were waited for; matrix products, arithmetic and copies ran while one was open for 1% of the time, Pallas kernels for 0%

profile of v1, /device:TPU:0, one launch (start us, length us, event | category | flops | bytes accessed | tf_op | source)
XLA Modules:
  0.0 232.5 jit_solution(4625745229432421067)
XLA Ops:
  0.6 0.8 copy.16.dt_ref
  1.4 1.0 copy-done.1
  2.5 0.8 copy-done.7
  3.3 0.8 copy-done.9
  4.2 0.7 copy-done.10
  4.8 2.4 %block_states.1 = bf16[32,208,128]{2,1,0:T(8,128)(2,1)} custom-call(bf16[128,2048]{1,0:T(8,128)(2,1)S(1)} %copy-done.1, bf16[128,256]{1,0:T(8,128)(2,1)S(1)} %copy-done.7, f32[128,16]{1,0:T(8,128)S(1)} %copy.16.dt_ref, f32[1,16]{1,0:T(1,128)S(1)} %bitcast.3, bf16[128,256]{1,0:T(8,128)(2,1)S(1)} %copy-done.9), custom_call_target="tpu_custom_call" | custom-call | flops 134217728 | bytes 4194304 | tf_op jit(solution)/shard_map/block_states/pallas_call | solution.py:316
  7.2 10.8 %all-to-all-start = ((bf16[32,208,128]{2,1,0:T(8,128)(2,1)}), bf16[32,208,128]{2,1,0:T(8,128)(2,1)S(1)}, u32[]{:S(2)}, u32[]{:S(2)}) async-start(bf16[32,208,128]{2,1,0:T(8,128)(2,1)} %block_states.1), calls=%async_computation | async-start | bytes 3407872 | tf_op jit(solution)/shard_map/all_to_all | solution.py:331
  18.1 0.1 slice_select_fusion
  18.2 7.7 %collective-permute-start = (bf16[256,1024]{1,0:T(8,128)(2,1)S(1)}, bf16[256,1024]{1,0:T(8,128)(2,1)S(1)}, u32[]{:S(2)}, u32[]{:S(2)}) collective-permute-start(bf16[256,1024]{1,0:T(8,128)(2,1)S(1)} %pad_maximum_fusion), channel_id=1, source_target_pairs={{0,124},{4,120},{8,116},{12,112},{16,108},{20,104},{24,100},{28,96... | collective-permute-start | bytes 1572872 | tf_op jit(solution)/shard_map/ppermute | solution.py:351
  25.8 29.5 %collective-permute-done.other_ref = bf16[256,1024]{1,0:T(8,128)(2,1)S(1)} collective-permute-done((bf16[256,1024]{1,0:T(8,128)(2,1)S(1)}, bf16[256,1024]{1,0:T(8,128)(2,1)S(1)}, u32[]{:S(2)}, u32[]{:S(2)}) %collective-permute-start) | collective-permute-done | bytes 524320 | tf_op jit(solution)/shard_map/ppermute | solution.py:351
  55.4 0.8 copy-done.17
  56.1 0.6 copy-done.13
  56.7 25.1 %probs.1 = (bf16[32,192,128]{2,1,0:T(8,128)(2,1)}, bf16[33,128,1024]{2,1,0:T(8,128)(2,1)}, bf16[2,1024,128]{2,1,0:T(8,128)(2,1)}, bf16[2,1024,128]{2,1,0:T(8,128)(2,1)}) custom-call(s32[1]{0:T(128)} %bitcast.at_ref, bf16[32,208,128]{2,1,0:T(8,128)(2,1)} %copy-done.13, bf16[128,2048]{1,0:T(8,128)(2,1)} %q_ref.1, bf16[128,2048]{1,0:T(8,128)(2,1)} %d_ref.1, ...), custom_call_target="tpu_custom_call" | custom-call | flops 4294967296 | bytes 16777216 | tf_op jit(solution)/shard_map/probs/pallas_call | solution.py:316
  81.8 0.0 copy-start.8
  81.8 0.0 copy-start.11
  81.8 0.0 copy-start.12
  81.8 28.8 %all_to_all.25.r2_ref = bf16[32,192,128]{2,1,0:T(8,128)(2,1)S(1)} all-to-all(bf16[32,192,128]{2,1,0:T(8,128)(2,1)} %get-tuple-element.19), channel_id=1, replica_groups=mesh['ctx'=32,'ch'=2,'section'=2] {'ctx'}, dimensions={0} | all-to-all | bytes 3145728 | tf_op jit(solution)/shard_map/all_to_all | solution.py:331
  110.7 2.0 values.1
  112.7 11.2 %all_to_all.26.r3_ref = bf16[4,128,512]{2,1,0:T(8,128)(2,1)S(1)} all-to-all(bf16[4,128,512]{2,1,0:T(8,128)(2,1)S(1)} %values.1), channel_id=1, replica_groups=mesh['ctx'=32,'ch'=2,'section'=2] {'ch','section'}, dimensions={0} | all-to-all | bytes 1048576 | tf_op jit(solution)/shard_map/all_to_all | solution.py:368
  123.9 5.4 %value_back.1 = (bf16[32,192,128]{2,1,0:T(8,128)(2,1)S(1)}, f32[128,2048]{1,0:T(8,128)S(1)}) custom-call(bf16[4,128,512]{2,1,0:T(8,128)(2,1)S(1)} %all_to_all.26.r3_ref, bf16[2048,1024]{1,0:T(8,128)(2,1)S(1)} %copy-done, bf16[128,256]{1,0:T(8,128)(2,1)S(1)} %copy-done.6, f32[128,16]{1,0:T(8,128)S(1)} %copy.16.dt_ref, f32[1,16]{1,0:T(1,128)S(1)} %bitcast.5), custom_call_target="tpu_custom_call" | custom-call | flops 1073741824 | bytes 8388608 | tf_op jit(solution)/shard_map/value_back/pallas_call | solution.py:316
  129.3 28.1 %all_to_all.27.r4_ref = bf16[32,192,128]{2,1,0:T(8,128)(2,1)} all-to-all(bf16[32,192,128]{2,1,0:T(8,128)(2,1)S(1)} %get-tuple-element.20), channel_id=1, replica_groups=mesh['ctx'=32,'ch'=2,'section'=2] {'ctx'}, dimensions={0} | all-to-all | bytes 3145728 | tf_op jit(solution)/shard_map/all_to_all | solution.py:331
  157.4 28.3 %attention_grads.1 = (bf16[32,192,128]{2,1,0:T(8,128)(2,1)}, f32[256,1024]{1,0:T(8,128)}, bf16[256,1024]{1,0:T(8,128)(2,1)}) custom-call(s32[1]{0:T(128)} %bitcast.at_ref, bf16[32,208,128]{2,1,0:T(8,128)(2,1)} %copy-done.13, bf16[32,192,128]{2,1,0:T(8,128)(2,1)} %all_to_all.27.r4_ref, bf16[33,128,1024]{2,1,0:T(8,128)(2,1)} %get-tuple-element.21.p_ref, ...), custom_call_target="tpu_custom_call" | custom-call | flops 4294967296 | bytes 16777216 | tf_op jit(solution)/shard_map/attention_grads/pallas_call | solution.py:316
  185.7 4.0 %all-to-all-start.4 = ((bf16[32,192,128]{2,1,0:T(8,128)(2,1)}), bf16[32,192,128]{2,1,0:T(8,128)(2,1)S(1)}, u32[]{:S(2)}, u32[]{:S(2)}) async-start(bf16[32,192,128]{2,1,0:T(8,128)(2,1)} %get-tuple-element.27), calls=%async_computation.4 | async-start | bytes 3145728 | tf_op jit(solution)/shard_map/all_to_all | solution.py:331
  189.7 0.0 copy-start.14
  189.7 7.9 %collective-permute-start.1 = (bf16[256,1024]{1,0:T(8,128)(2,1)}, bf16[256,1024]{1,0:T(8,128)(2,1)S(1)}, u32[]{:S(2)}, u32[]{:S(2)}) collective-permute-start(bf16[256,1024]{1,0:T(8,128)(2,1)} %get-tuple-element.24), channel_id=1, source_target_pairs={{0,124},{4,120},{8,116},{12,112},{16,108},{20,104},{24,100},{28,96... | collective-permute-start | bytes 1572872 | tf_op jit(solution)/shard_map/ppermute | solution.py:380
  197.6 27.1 %collective-permute-done.1 = bf16[256,1024]{1,0:T(8,128)(2,1)S(1)} collective-permute-done((bf16[256,1024]{1,0:T(8,128)(2,1)}, bf16[256,1024]{1,0:T(8,128)(2,1)S(1)}, u32[]{:S(2)}, u32[]{:S(2)}) %collective-permute-start.1) | collective-permute-done | bytes 524320 | tf_op jit(solution)/shard_map/ppermute | solution.py:380
  224.6 0.1 convert_element_type.3
  224.8 0.3 maximum_select_fusion
  225.1 1.5 fusion
  226.6 1.0 copy-done.3
  227.6 1.2 copy-done.5
  228.8 3.7 %mixer_grads.1 = (f32[128,2048]{1,0:T(8,128)}, f32[128,256]{1,0:T(8,128)}, f32[128,256]{1,0:T(8,128)}, f32[128,256]{1,0:T(8,128)}) custom-call(bf16[128,2048]{1,0:T(8,128)(2,1)S(1)} %copy-done.3, bf16[128,256]{1,0:T(8,128)(2,1)S(1)} %copy-done.8, bf16[128,256]{1,0:T(8,128)(2,1)S(1)} %copy-done.6, f32[128,16]{1,0:T(8,128)S(1)} %copy.16.dt_ref, ...), custom_call_target="tpu_custom_call" | custom-call | flops 536870912 | bytes 8388608 | tf_op jit(solution)/shard_map/mixer_grads/pallas_call | solution.py:316
  (27 shorter events, 0.1 us)
Async XLA Ops:
  1.4 1.0 copy-start.1
  2.5 0.8 copy-start.7
  3.3 0.8 copy-start.9
  4.2 0.7 copy-start.10
  7.2 10.9 %copy-start.15 = (bf16[128,2048]{1,0:T(8,128)(2,1)S(1)}, bf16[128,2048]{1,0:T(8,128)(2,1)}, u32[]{:S(2)}) copy-start(bf16[128,2048]{1,0:T(8,128)(2,1)} %q_ref.1) | copy-start | bytes 1572868
  7.2 10.9 %copy-start.16 = (bf16[128,2048]{1,0:T(8,128)(2,1)S(1)}, bf16[128,2048]{1,0:T(8,128)(2,1)}, u32[]{:S(2)}) copy-start(bf16[128,2048]{1,0:T(8,128)(2,1)} %d_ref.1) | copy-start | bytes 1572868
  7.2 48.2 %all-to-all-start = ((bf16[32,208,128]{2,1,0:T(8,128)(2,1)}), bf16[32,208,128]{2,1,0:T(8,128)(2,1)S(1)}, u32[]{:S(2)}, u32[]{:S(2)}) async-start(bf16[32,208,128]{2,1,0:T(8,128)(2,1)} %block_states.1), calls=%async_computation | async-start | bytes 3407872 | tf_op jit(solution)/shard_map/all_to_all | solution.py:331
  18.2 37.2 %collective-permute-start = (bf16[256,1024]{1,0:T(8,128)(2,1)S(1)}, bf16[256,1024]{1,0:T(8,128)(2,1)S(1)}, u32[]{:S(2)}, u32[]{:S(2)}) collective-permute-start(bf16[256,1024]{1,0:T(8,128)(2,1)S(1)} %pad_maximum_fusion), channel_id=1, source_target_pairs={{0,124},{4,120},{8,116},{12,112},{16,108},{20,104},{24,100},{28,96... | collective-permute-start | bytes 1572872 | tf_op jit(solution)/shard_map/ppermute | solution.py:351
  55.3 0.8 copy-start.17
  55.4 1.4 copy-start.13
  56.7 53.9 %copy-start = (bf16[2048,1024]{1,0:T(8,128)(2,1)S(1)}, bf16[2048,1024]{1,0:T(8,128)(2,1)}, u32[]{:S(2)}) copy-start(bf16[2048,1024]{1,0:T(8,128)(2,1)} %w_ref.3) | copy-start | bytes 12582916
  81.8 28.9 %copy-start.2 = (bf16[128,2048]{1,0:T(8,128)(2,1)S(1)}, bf16[128,2048]{1,0:T(8,128)(2,1)}, u32[]{:S(2)}) copy-start(bf16[128,2048]{1,0:T(8,128)(2,1)} %x_ref.5) | copy-start | bytes 1572868
  81.8 28.9 %copy-start.6 = (bf16[128,256]{1,0:T(8,128)(2,1)S(1)}, bf16[128,256]{1,0:T(8,128)(2,1)}, u32[]{:S(2)}) copy-start(bf16[128,256]{1,0:T(8,128)(2,1)} %c_ref.5) | copy-start | bytes 196612
  81.8 28.9 %copy-start.8 = (bf16[128,256]{1,0:T(8,128)(2,1)S(1)}, bf16[128,256]{1,0:T(8,128)(2,1)}, u32[]{:S(2)}) copy-start(bf16[128,256]{1,0:T(8,128)(2,1)} %b_ref.5) | copy-start | bytes 196612
  81.8 28.9 %copy-start.11 = (f32[16]{0:T(128)S(1)}, f32[16]{0:T(128)}, u32[]{:S(2)}) copy-start(f32[16]{0:T(128)} %param.14) | copy-start | bytes 196
  81.8 28.8 %copy-start.12 = (f32[16]{0:T(128)S(1)}, f32[16]{0:T(128)}, u32[]{:S(2)}) copy-start(f32[16]{0:T(128)} %param.15) | copy-start | bytes 196
  129.3 28.1 %copy-start.4 = (f32[128,2048]{1,0:T(8,128)}, f32[128,2048]{1,0:T(8,128)S(1)}, u32[]{:S(2)}) copy-start(f32[128,2048]{1,0:T(8,128)S(1)} %get-tuple-element.26.dy_ref) | copy-start | bytes 3145732
  185.7 40.8 %all-to-all-start.4 = ((bf16[32,192,128]{2,1,0:T(8,128)(2,1)}), bf16[32,192,128]{2,1,0:T(8,128)(2,1)S(1)}, u32[]{:S(2)}, u32[]{:S(2)}) async-start(bf16[32,192,128]{2,1,0:T(8,128)(2,1)} %get-tuple-element.27), calls=%async_computation.4 | async-start | bytes 3145728 | tf_op jit(solution)/shard_map/all_to_all | solution.py:331
  189.7 35.0 %copy-start.14 = (f32[256,1024]{1,0:T(8,128)S(1)}, f32[256,1024]{1,0:T(8,128)}, u32[]{:S(2)}) copy-start(f32[256,1024]{1,0:T(8,128)} %get-tuple-element.25) | copy-start | bytes 3145732
  189.7 34.9 %collective-permute-start.1 = (bf16[256,1024]{1,0:T(8,128)(2,1)}, bf16[256,1024]{1,0:T(8,128)(2,1)S(1)}, u32[]{:S(2)}, u32[]{:S(2)}) collective-permute-start(bf16[256,1024]{1,0:T(8,128)(2,1)} %get-tuple-element.24), channel_id=1, source_target_pairs={{0,124},{4,120},{8,116},{12,112},{16,108},{20,104},{24,100},{28,96... | collective-permute-start | bytes 1572872 | tf_op jit(solution)/shard_map/ppermute | solution.py:380
  226.6 1.0 copy-start.3
  227.6 1.2 copy-start.5

commit v2 on v1

--- a/solution.py
+++ b/solution.py
@@ -85,17 +85,33 @@
     return jnp.exp(parts[0:1] + parts[1:2] + parts[2:3])
 
 
+def steps_of(n, step, init):
+    whole = n // 4
+    init = lax.fori_loop(0, whole, lambda i, c: step(i * 4, 4, c), init)
+    pairs = (n - whole * 4) // 2
+    init = lax.fori_loop(0, pairs, lambda i, c: step(whole * 4, 2, c), init)
+    return lax.fori_loop(whole * 4 + pairs * 2, n, lambda i, c: step(i, 1, c), init)
+
+
+def rows_of(ref, j, u, first):
+    return jnp.concatenate([ref[j + n, first : first + T, :] for n in range(u)], axis=0)
+
+
+def quarter(c):
+    return slice(c * 256, (c + 1) * 256)
+
+
+def fold(x):
+    return x.reshape(-1, 8, 256)
+
+
 def probs_kernel(
-    at_ref, r1_ref, q_ref, d_ref, other_ref, pay_ref, p_ref, qs_ref, ds_ref, s_sc, dv_sc
+    at_ref, r1_ref, q_ref, d_ref, other_ref, pay_ref, p_hbm, qs_ref, ds_ref,
+    s_sc, dv_sc, qt_sc, sem
 ):
     at = at_ref[0]
     upper = (at >= 16).astype(jnp.int32)
     low = jnp.minimum(at, 31 - at)
-
-    run = jnp.zeros((SR, T), F32)
-    for c in range(32):
-        pay_ref[c, 0:SR, :] = run.astype(BF)
-        run = decay_of(r1_ref, c) * run + r1_ref[c, 0:SR, :].astype(F32)
 
     for h in range(GH):
         own = pl.ds(pl.multiple_of(upper * 1024 + h * T, T), T)
@@ -103,6 +119,8 @@
         ds_ref[upper, head(h), :] = d_ref[:, own]
         qs_ref[1 - upper, head(h), :] = other_ref[0:T, head(h)]
         ds_ref[1 - upper, head(h), :] = other_ref[T : 2 * T, head(h)]
+        qt_sc[upper, :, head(h)] = jnp.transpose(q_ref[:, own])
+        qt_sc[1 - upper, :, head(h)] = jnp.transpose(other_ref[0:T, head(h)])
 
     dv_sc[...] = jnp.zeros_like(dv_sc)
     key = lax.broadcasted_iota(jnp.int32, (T, 256), 0)
@@ -113,50 +131,61 @@
         count = low if sel == 0 else 31 - low
         base = 0 if sel == 0 else low + 1
 
-        def scores(j, top, diag, sel=sel, base=base):
-            k = r1_ref[j, SR + DR : SR + DR + T, :]
+        def scores(j, u, top, diag=False, sel=sel, base=base):
+            k = rows_of(r1_ref, j, u, SR + DR)
             tops = []
             for c in range(4):
-                cols = slice(c * 256, (c + 1) * 256)
-                s = mm(k, qs_ref[sel, cols, :], NT)
+                s = mm(k, qt_sc[sel, :, quarter(c)])
                 if diag:
                     s = jnp.where(seen, s, NEG)
-                s_sc[base + j, :, cols] = s
-                tops.append(jnp.maximum(top[c], jnp.max(s.reshape(16, 8, 256), axis=0)))
+                s_sc[pl.ds(base + j, u), :, quarter(c)] = s.reshape(u, T, 256)
+                tops.append(jnp.maximum(top[c], jnp.max(fold(s), axis=0)))
             return tuple(tops)
 
         top = tuple(jnp.full((8, 256), NEG, F32) for _ in range(4))
-        top = lax.fori_loop(0, count, lambda j, t: scores(j, t, False), top)
-        top = scores(count, top, True)
+        top = steps_of(count, scores, top)
+        top = scores(count, 1, top, True)
         peak = [jnp.max(t, axis=0, keepdims=True) for t in top]
 
-        def weigh(j, tot, base=base, peak=peak):
+        def weigh(j, u, tot, base=base, peak=peak):
             tots = []
             for c in range(4):
-                cols = slice(c * 256, (c + 1) * 256)
-                p = jnp.exp((s_sc[base + j, :, cols] - peak[c]) * SCALE)
-                s_sc[base + j, :, cols] = p
-                tots.append(tot[c] + jnp.sum(p.reshape(16, 8, 256), axis=0))
+                p = jnp.exp((s_sc[pl.ds(base + j, u), :, quarter(c)] - peak[c]) * SCALE)
+                tots.append(tot[c] + jnp.sum(fold(p), axis=0))
             return tuple(tots)
 
         tot = tuple(jnp.zeros((8, 256), F32) for _ in range(4))
-        tot = lax.fori_loop(0, count + 1, weigh, tot)
-        inv = [1.0 / jnp.sum(t, axis=0, keepdims=True) for t in tot]
-
-        def spread(j, none, sel=sel, base=base, inv=inv):
-            acc = dv_sc[j]
+        tot = steps_of(count + 1, weigh, tot)
+        shift = [
+            peak[c] * SCALE + jnp.log(jnp.sum(tot[c], axis=0, keepdims=True)) for c in range(4)
+        ]
+
+        def spread(j, u, none, sel=sel, base=base, shift=shift):
+            ps = []
+            at_b = pl.ds(base + j, u)
             for c in range(4):
-                cols = slice(c * 256, (c + 1) * 256)
-                p = (s_sc[base + j, :, cols] * inv[c]).astype(BF)
-                p_ref[base + j, :, cols] = p
-                acc = acc + mm(p, ds_ref[sel, cols, :])
-            dv_sc[j] = acc
+                p = jnp.exp(s_sc[at_b, :, quarter(c)] * SCALE - shift[c])
+                s_sc[at_b, :, quarter(c)] = p
+                ps.append(p.astype(BF).reshape(u * T, 256))
+            term = mm(jnp.concatenate(ps, axis=1), ds_ref[sel])
+            dv_sc[pl.ds(j, u)] = dv_sc[pl.ds(j, u)] + term.reshape(u, T, T)
+            pltpu.make_async_copy(s_sc.at[at_b], p_hbm.at[at_b], sem).start()
             return none
 
-        lax.fori_loop(0, count + 1, spread, 0)
-
+        steps_of(count + 1, spread, 0)
+
+    run = jnp.zeros((SR, T), F32)
+    for c in range(32):
+        pay_ref[c, 0:SR, :] = run.astype(BF)
+        run = decay_of(r1_ref, c) * run + r1_ref[c, 0:SR, :].astype(F32)
     for c in range(32):
         pay_ref[c, SR : SR + T, :] = dv_sc[c].astype(BF)
+    pltpu.make_async_copy(s_sc, p_hbm, sem).wait()
+
+
+def split(x):
+    big = x.astype(BF)
+    return big, (x - big.astype(F32)).astype(BF)
 
 
 def values_kernel(
@@ -173,7 +202,8 @@
             mix = cb * jnp.exp(jnp.where(lower, gap, NEG)) * dt_t[h : h + 1, :]
             x = x_ref[:, head(h)]
             enter = jnp.concatenate([r2_ref[2 * h, 0:SR, :], r2_ref[2 * h + 1, 0:SR, :]], 0)
-            y = mm(mix.astype(BF), x) + skip_ref[:, h : h + 1] * x.astype(F32)
+            mix, rest = split(mix)
+            y = mm(mix, x) + mm(rest, x) + skip_ref[:, h : h + 1] * x.astype(F32)
             y = y + grow[:, h : h + 1] * mm(c_ref[:, head(g)], enter, NT)
             y_sc[:, head(h)] = y.astype(BF)
     dv = []
@@ -183,20 +213,22 @@
             acc = acc + r2_ref[16 * k + s, SR : SR + T, :].astype(F32)
         dv.append(acc.astype(BF))
     for d in range(4):
-        cols = slice(d * 256, (d + 1) * 256)
-        out_ref[d, :, 0:256] = mm(y_sc[...], w_ref[:, cols]).astype(BF)
-        out_ref[d, :, 256:384] = dv[0]
-        out_ref[d, :, 384:512] = dv[1]
+        big, rest = split(mm(y_sc[...], w_ref[:, quarter(d)]))
+        out_ref[d, :, 0:256] = big
+        out_ref[d, :, 256:512] = rest
+        out_ref[d, :, 512:640] = dv[0]
+        out_ref[d, :, 640:768] = dv[1]
 
 
 def back_kernel(r3_ref, w_ref, c_ref, dt_ref, a_ref, pay_ref, dy_ref):
-    values = r3_ref[0, :, 0:256].astype(F32)
+    values = r3_ref[0, :, 0:256].astype(F32) + r3_ref[0, :, 256:512].astype(F32)
     for s in range(1, 4):
         values = values + r3_ref[s, :, 0:256].astype(F32)
+        values = values + r3_ref[s, :, 256:512].astype(F32)
     values = values.astype(BF)
     for d in range(32):
         pay_ref[d, SR : SR + T, :] = values[:, head(d // 16)]
-    vg = jnp.concatenate([r3_ref[s, :, 256:512] for s in range(4)], axis=1)
+    vg = jnp.concatenate([r3_ref[s, :, 512:768] for s in range(4)], axis=1)
     grow = jnp.exp(sums_by_token(dt_ref, a_ref))
     for h in range(NH):
         dy = mm(vg, w_ref[head(h), :], NT)
@@ -207,18 +239,23 @@
 
 
 def grads_kernel(
-    at_ref, r1_ref, r4_ref, p_ref, qs_ref, ds_ref, pay_ref, o_ref, send_ref,
-    dp_sc, o_sc, dq_sc, dk_sc
+    at_ref, r1_ref, r4_ref, qs_ref, ds_ref, p_hbm, pay_ref, o_ref, send_ref,
+    p_sc, dp_sc, o_sc, dq_sc, dk_sc, dt_sc, sem
 ):
     at = at_ref[0]
     upper = (at >= 16).astype(jnp.int32)
     low = jnp.minimum(at, 31 - at)
+    for b in range(33):
+        pltpu.make_async_copy(p_hbm.at[b], p_sc.at[b], sem.at[b]).start()
 
     run = jnp.zeros((SR, T), F32)
     for c in range(31, -1, -1):
         pay_ref[c, 0:SR, :] = run.astype(BF)
         run = decay_of(r1_ref, c) * run + r4_ref[c, 0:SR, :].astype(F32)
 
+    for sel in range(2):
+        for h in range(GH):
+            dt_sc[sel, :, head(h)] = jnp.transpose(ds_ref[sel, head(h), :])
     dk_sc[...] = jnp.zeros_like(dk_sc)
     o_sc[...] = jnp.zeros_like(o_sc)
     dq_sc[...] = jnp.zeros_like(dq_sc)
@@ -226,36 +263,41 @@
         count = low if sel == 0 else 31 - low
         base = 0 if sel == 0 else low + 1
 
-        def first(j, delta, sel=sel, base=base):
-            v = r4_ref[j, SR : SR + T, :]
+        def first(j, u, delta, sel=sel, base=base):
+            for n in range(u):
+                b = base + j + n
+                pltpu.make_async_copy(p_hbm.at[b], p_sc.at[b], sem.at[b]).wait()
+            at_b = pl.ds(base + j, u)
+            v = rows_of(r4_ref, j, u, SR)
+            v_t = jnp.transpose(v)
             deltas = []
             for c in range(4):
-                cols = slice(c * 256, (c + 1) * 256)
-                p = p_ref[base + j, :, cols]
-                dp = mm(v, ds_ref[sel, cols, :], NT)
-                dp_sc[base + j, :, cols] = dp
+                p = p_sc[at_b, :, quarter(c)].astype(BF).reshape(u * T, 256)
+                dp = mm(v, dt_sc[sel, :, quarter(c)])
+                dp_sc[at_b, :, quarter(c)] = dp.reshape(u, T, 256)
                 term = p.astype(F32) * dp
-                deltas.append(delta[c] + jnp.sum(term.reshape(16, 8, 256), axis=0))
-                o_sc[sel, :, cols] += mm(v, p, TN)
+                deltas.append(delta[c] + jnp.sum(fold(term), axis=0))
+                o_sc[sel, :, quarter(c)] += mm(v_t, p)
             return tuple(deltas)
 
         delta = tuple(jnp.zeros((8, 256), F32) for _ in range(4))
-        delta = lax.fori_loop(0, count + 1, first, delta)
+        delta = steps_of(count + 1, first, delta)
         delta = [jnp.sum(t, axis=0, keepdims=True) for t in delta]
 
-        def second(j, none, sel=sel, base=base, delta=delta):
-            k = r1_ref[j, SR + DR : SR + DR + T, :]
-            acc = dk_sc[j]
+        def second(j, u, none, sel=sel, base=base, delta=delta):
+            at_b = pl.ds(base + j, u)
+            k_t = jnp.transpose(rows_of(r1_ref, j, u, SR + DR))
+            parts = []
             for c in range(4):
-                cols = slice(c * 256, (c + 1) * 256)
-                p = p_ref[base + j, :, cols].astype(F32)
-                ds = (p * (dp_sc[base + j, :, cols] - delta[c])).astype(BF)
-                dq_sc[sel, :, cols] += mm(k, ds, TN)
-                acc = acc + mm(ds, qs_ref[sel, cols, :])
-            dk_sc[j] = acc
+                ds = p_sc[at_b, :, quarter(c)] * (dp_sc[at_b, :, quarter(c)] - delta[c])
+                ds = ds.astype(BF).reshape(u * T, 256)
+                dq_sc[sel, :, quarter(c)] += mm(k_t, ds)
+                parts.append(ds)
+            term = mm(jnp.concatenate(parts, axis=1), qs_ref[sel])
+            dk_sc[pl.ds(j, u)] = dk_sc[pl.ds(j, u)] + term.reshape(u, T, T)
             return none
 
-        lax.fori_loop(0, count + 1, second, 0)
+        steps_of(count + 1, second, 0)
 
     for c in range(32):
         pay_ref[c, SR : SR + T, :] = dk_sc[c].astype(BF)
@@ -268,21 +310,18 @@
         ).astype(BF)
 
 
-def final_kernel(
-    x_ref, b_ref, c_ref, dt_ref, a_ref, skip_ref, dy_ref, r2_ref, r5_ref,
-    gx_ref, gb_ref, gc_ref, gk_ref
+def local_kernel(
+    x_ref, b_ref, c_ref, dt_ref, a_ref, skip_ref, dy_ref, r2_ref, gx_ref, gb_ref, gc_ref
 ):
     cum = sums_by_token(dt_ref, a_ref)
     cum_t, dt_t = sums_by_head(dt_ref, a_ref)
     grow = jnp.exp(cum)
-    weight = jnp.exp(cum[T - 1 : T, :] - cum) * dt_ref[...]
     lower = lower_tri()
     for g in range(2):
         b = b_ref[:, head(g)]
         cc = c_ref[:, head(g)]
         cb = mm(cc, b, NT)
         mixed = jnp.zeros((T, T), F32)
-        gb = jnp.zeros((T, T), F32)
         gc = jnp.zeros((T, T), F32)
         for h in range(g * GH, (g + 1) * GH):
             gap = cum[:, h : h + 1] - cum_t[h : h + 1, :]
@@ -292,15 +331,27 @@
             dy = dy_ref[:, head(h)]
             dyb = dy.astype(BF)
             enter = jnp.concatenate([r2_ref[2 * h, 0:SR, :], r2_ref[2 * h + 1, 0:SR, :]], 0)
-            sg = jnp.concatenate([r5_ref[2 * h, 0:SR, :], r5_ref[2 * h + 1, 0:SR, :]], 0)
-            gx = mm(mix, dyb, TN) + skip_ref[:, h : h + 1] * dy
-            gx_ref[:, head(h)] = gx + weight[:, h : h + 1] * mm(b, sg, NT)
+            gx_ref[:, head(h)] = mm(mix, dyb, TN) + skip_ref[:, h : h + 1] * dy
             mixed = mixed + mm(dyb, x, NT) * decay
-            gb = gb + weight[:, h : h + 1] * mm(x, sg)
             gc = gc + grow[:, h : h + 1] * mm(dyb, enter)
         mixed = mixed.astype(BF)
-        gb_ref[:, head(g)] = gb + mm(mixed, cc, TN)
+        gb_ref[:, head(g)] = mm(mixed, cc, TN)
         gc_ref[:, head(g)] = gc + mm(mixed, b)
+
+
+def final_kernel(
+    x_ref, b_ref, dt_ref, a_ref, gx0_ref, gb0_ref, r5_ref, gx_ref, gb_ref, gk_ref
+):
+    cum = sums_by_token(dt_ref, a_ref)
+    weight = jnp.exp(cum[T - 1 : T, :] - cum) * dt_ref[...]
+    for g in range(2):
+        b = b_ref[:, head(g)]
+        gb = gb0_ref[:, head(g)]
+        for h in range(g * GH, (g + 1) * GH):
+            sg = jnp.concatenate([r5_ref[2 * h, 0:SR, :], r5_ref[2 * h + 1, 0:SR, :]], 0)
+            gx_ref[:, head(h)] = gx0_ref[:, head(h)] + weight[:, h : h + 1] * mm(b, sg, NT)
+            gb = gb + weight[:, h : h + 1] * mm(x_ref[:, head(h)], sg)
+        gb_ref[:, head(g)] = gb
     for k in range(2):
         acc = r5_ref[16 * k, SR : SR + T, :].astype(F32)
         for s in range(1, 16):
@@ -310,16 +361,18 @@
 
 VM = pl.BlockSpec(memory_space=pltpu.VMEM)
 SM = pl.BlockSpec(memory_space=pltpu.SMEM)
-
-
-def call(kernel, outs, scratch, name, mib, flops, nbytes, *args):
+ANY = pl.BlockSpec(memory_space=pl.ANY)
+
+
+def call(kernel, outs, scratch, name, mib, flops, nbytes, *args, far_in=(), far_out=()):
+    places = [SM if a.dtype == jnp.int32 else VM for a in args]
     return pl.pallas_call(
         kernel,
         name=name,
         out_shape=[jax.ShapeDtypeStruct(s, d) for s, d in outs],
-        in_specs=[SM if a.dtype == jnp.int32 else VM for a in args],
-        out_specs=[VM] * len(outs),
-        scratch_shapes=[pltpu.VMEM(s, d) for s, d in scratch],
+        in_specs=[ANY if n in far_in else place for n, place in enumerate(places)],
+        out_specs=[ANY if n in far_out else VM for n in range(len(outs))],
+        scratch_shapes=scratch,
         cost_estimate=pl.CostEstimate(
             flops=flops, bytes_accessed=nbytes, transcendentals=0
         ),
@@ -356,34 +409,49 @@
     r1 = over_ctx(pay1)
     pay2, probs, qs, ds = call(
         probs_kernel,
-        [((32, SR + T, T), BF), ((33, T, 1024), BF), ((2, 1024, T), BF), ((2, 1024, T), BF)],
-        [((33, T, 1024), F32), ((32, T, T), F32)],
-        "probs", 56, 1 << 32, 1 << 24, at1, r1, queries, out_grad, other,
+        [((32, SR + T, T), BF), ((33, T, 1024), F32), ((2, 1024, T), BF), ((2, 1024, T), BF)],
+        [
+            pltpu.VMEM((33, T, 1024), F32), pltpu.VMEM((32, T, T), F32),
+            pltpu.VMEM((2, T, 1024), BF), pltpu.SemaphoreType.DMA,
+        ],
+        "probs", 40, 1 << 32, 1 << 25, at1, r1, queries, out_grad, other, far_out=(1,),
     )
     r2 = over_ctx(pay2)
     (pay3,) = call(
-        values_kernel, [((4, T, 512), BF)], [((T, 2048), BF)], "values", 32, 1 << 30, 1 << 23,
+        values_kernel, [((4, T, 768), BF)], [pltpu.VMEM((T, 2048), BF)], "values", 24,
+        1 << 30, 1 << 23,
         mamba_x, mamba_b, mamba_c, step_dt, a_row, skip_row, r2, value_weight,
     )
     r3 = lax.all_to_all(pay3, ("ch", "section"), 0, 0, tiled=True)
     pay4, dy = call(
-        back_kernel, [((32, SR + T, T), BF), ((T, 2048), F32)], [], "value_back", 32, 1 << 30,
+        back_kernel, [((32, SR + T, T), BF), ((T, 2048), F32)], [], "value_back", 24, 1 << 30,
         1 << 23, r3, value_weight, mamba_c, step_dt, a_row,
     )
     r4 = over_ctx(pay4)
+    gx0, gb0, grad_c = call(
+        local_kernel,
+        [((T, 2048), F32), ((T, 256), F32), ((T, 256), F32)], [], "mixer_local", 24,
+        1 << 29, 1 << 23,
+        mamba_x, mamba_b, mamba_c, step_dt, a_row, skip_row, dy, r2,
+    )
     pay5, kept, send = call(
         grads_kernel,
         [((32, SR + T, T), BF), ((256, 1024), F32), ((256, 1024), BF)],
-        [((33, T, 1024), F32), ((2, T, 1024), F32), ((2, T, 1024), F32), ((32, T, T), F32)],
-        "attention_grads", 60, 1 << 32, 1 << 24, at1, r1, r4, probs, qs, ds,
+        [
+            pltpu.VMEM((33, T, 1024), F32), pltpu.VMEM((33, T, 1024), F32),
+            pltpu.VMEM((2, T, 1024), F32), pltpu.VMEM((2, T, 1024), F32),
+            pltpu.VMEM((32, T, T), F32), pltpu.VMEM((2, T, 1024), BF),
+            pltpu.SemaphoreType.DMA((33,)),
+        ],
+        "attention_grads", 56, 1 << 32, 1 << 25, at1, r1, r4, qs, ds, probs, far_in=(5,),
     )
     back = lax.ppermute(send, "ctx", swap)
     r5 = over_ctx(pay5)
-    grad_x, grad_b, grad_c, grad_k = call(
+    grad_x, grad_b, grad_k = call(
         final_kernel,
-        [((T, 2048), F32), ((T, 256), F32), ((T, 256), F32), ((T, 256), F32)],
-        [], "mixer_grads", 32, 1 << 29, 1 << 23,
-        mamba_x, mamba_b, mamba_c, step_dt, a_row, skip_row, dy, r2, r5,
+        [((T, 2048), F32), ((T, 256), F32), ((T, 256), F32)],
+        [], "mixer_grads", 24, 1 << 29, 1 << 23,
+        mamba_x, mamba_b, step_dt, a_row, gx0, gb0, r5,
     )
     back = back.astype(F32)
     whole = jnp.where(

time: 233 us -> 213 us (0.914)
  Pallas kernels: 66.8 us -> 46.5 us
  waiting for transfers between devices: 56.6 us -> 53 us
    pallas_call x6 -> x7, Pallas kernels: 66.8 us -> 46.5 us  [call(): pl.pallas_call(kernel, name=name, out_shape=[jax.ShapeDtypeStruct(s, d) f...]
    ppermute x1, waiting for transfers between devices: 27.1 us -> 23.5 us  [body(): back = lax.ppermute(send, 'ctx', swap)]
    all_to_all x1, blocking collectives: 11.2 us -> 14.1 us  [body(): r3 = lax.all_to_all(pay3, ('ch', 'section'), 0, 0, tiled=True)]
    unnamed x37 -> x41, local copies, waits for them, and re-layouts: 7.85 us -> 8.51 us
  transfers between devices with their start and end apart: 4 -> 4, of which waited for: 2 -> 2; matrix products, arithmetic and copies ran while one was open for 1% -> 1% of each run, Pallas kernels for 0% -> 1%
where the time goes in v2:
time: 213 us; the launch traced here: 212 us
  blocking collectives  70.1 us (33%)
  waiting for transfers between devices  53 us (25%)
  Pallas kernels  46.5 us (22%)
  starting transfers between devices  31.1 us (15%)
  local copies, waits for them, and re-layouts  9.97 us (5%)
    all_to_all x2, blocking collectives, over_ctx(): return lax.all_to_all(pay, 'ctx', 0, 0, tiled=True)  56 us
    pallas_call x7, Pallas kernels, call(): pl.pallas_call(kernel, name=name, out_shape=[jax.ShapeDtypeStruct(s, d) f...  46.5 us
    ppermute x1, waiting for transfers between devices, body(): other = lax.ppermute(away, 'ctx', swap)  29.5 us
    ppermute x1, waiting for transfers between devices, body(): back = lax.ppermute(send, 'ctx', swap)  23.5 us
    all_to_all x2, starting transfers between devices, over_ctx(): return lax.all_to_all(pay, 'ctx', 0, 0, tiled=True)  15.6 us
    all_to_all x1, blocking collectives, body(): r3 = lax.all_to_all(pay3, ('ch', 'section'), 0, 0, tiled=True)  14.1 us
    unnamed x41, local copies, waits for them, and re-layouts  8.51 us
    ppermute x1, starting transfers between devices, body(): back = lax.ppermute(send, 'ctx', swap)  7.84 us
  transfers between devices with their start and end apart: 4, of which 2 were waited for; matrix products, arithmetic and copies ran while one was open for 1% of the time, Pallas kernels for 1%

profile of v2, /device:TPU:0, one launch (start us, length us, event | category | flops | bytes accessed | tf_op | source)
XLA Modules:
  0.0 212.0 jit_solution(10834982691850417724)
XLA Ops:
  0.6 0.8 copy.16.dt_ref
  1.4 1.0 copy-done.1
  2.5 0.8 copy-done.4
  3.3 0.8 copy-done.13
  4.2 0.7 copy-done.14
  4.8 2.4 %block_states.1 = bf16[32,208,128]{2,1,0:T(8,128)(2,1)} custom-call(bf16[128,2048]{1,0:T(8,128)(2,1)S(1)} %copy-done.1, bf16[128,256]{1,0:T(8,128)(2,1)S(1)} %copy-done.4, f32[128,16]{1,0:T(8,128)S(1)} %copy.16.dt_ref, f32[1,16]{1,0:T(1,128)S(1)} %bitcast.3, bf16[128,256]{1,0:T(8,128)(2,1)S(1)} %copy-done.13), custom_call_target="tpu_custom_call" | custom-call | flops 134217728 | bytes 4194304 | tf_op jit(solution)/shard_map/block_states/pallas_call | solution.py:369
  7.2 10.8 %all-to-all-start = ((bf16[32,208,128]{2,1,0:T(8,128)(2,1)}), bf16[32,208,128]{2,1,0:T(8,128)(2,1)S(1)}, u32[]{:S(2)}, u32[]{:S(2)}) async-start(bf16[32,208,128]{2,1,0:T(8,128)(2,1)} %block_states.1), calls=%async_computation | async-start | bytes 3407872 | tf_op jit(solution)/shard_map/all_to_all | solution.py:384
  18.1 0.1 slice_select_fusion
  18.2 7.7 %collective-permute-start = (bf16[256,1024]{1,0:T(8,128)(2,1)S(1)}, bf16[256,1024]{1,0:T(8,128)(2,1)S(1)}, u32[]{:S(2)}, u32[]{:S(2)}) collective-permute-start(bf16[256,1024]{1,0:T(8,128)(2,1)S(1)} %pad_maximum_fusion), channel_id=1, source_target_pairs={{0,124},{4,120},{8,116},{12,112},{16,108},{20,104},{24,100},{28,96... | collective-permute-start | bytes 1572872 | tf_op jit(solution)/shard_map/ppermute | solution.py:404
  25.9 29.5 %collective-permute-done.other_ref = bf16[256,1024]{1,0:T(8,128)(2,1)S(1)} collective-permute-done((bf16[256,1024]{1,0:T(8,128)(2,1)S(1)}, bf16[256,1024]{1,0:T(8,128)(2,1)S(1)}, u32[]{:S(2)}, u32[]{:S(2)}) %collective-permute-start) | collective-permute-done | bytes 524320 | tf_op jit(solution)/shard_map/ppermute | solution.py:404
  55.4 0.8 copy-done.17
  56.1 1.0 copy-done.18
  57.2 14.1 %probs.1 = (bf16[32,192,128]{2,1,0:T(8,128)(2,1)S(1)}, f32[33,128,1024]{2,1,0:T(8,128)}, bf16[2,1024,128]{2,1,0:T(8,128)(2,1)S(1)}, bf16[2,1024,128]{2,1,0:T(8,128)(2,1)S(1)}) custom-call(s32[1]{0:T(128)} %bitcast.at_ref, bf16[32,208,128]{2,1,0:T(8,128)(2,1)S(1)} %all-to-all-done.r1_ref, bf16[128,2048]{1,0:T(8,128)(2,1)S(1)} %copy-done.11, ...), custom_call_target="tpu_custom_call" | custom-call | flops 4294967296 | bytes 33554432 | tf_op jit(solution)/shard_map/probs/pallas_call | solution.py:369
  71.3 1.2 copy-done.3
  72.5 0.0 copy-start.8
  72.5 0.0 copy-start.15
  72.6 0.0 copy-start.16
  72.6 27.9 %all_to_all.25.r2_ref = bf16[32,192,128]{2,1,0:T(8,128)(2,1)S(1)} all-to-all(bf16[32,192,128]{2,1,0:T(8,128)(2,1)S(1)} %get-tuple-element.21), channel_id=1, replica_groups=mesh['ctx'=32,'ch'=2,'section'=2] {'ctx'}, dimensions={0} | all-to-all | bytes 3145728 | tf_op jit(solution)/shard_map/all_to_all | solution.py:384
  100.5 2.1 values.1
  102.6 14.1 %all_to_all.26.r3_ref = bf16[4,128,768]{2,1,0:T(8,128)(2,1)S(1)} all-to-all(bf16[4,128,768]{2,1,0:T(8,128)(2,1)S(1)} %values.1), channel_id=1, replica_groups=mesh['ctx'=32,'ch'=2,'section'=2] {'ch','section'}, dimensions={0} | all-to-all | bytes 1572864 | tf_op jit(solution)/shard_map/all_to_all | solution.py:425
  116.7 5.4 %value_back.1 = (bf16[32,192,128]{2,1,0:T(8,128)(2,1)S(1)}, f32[128,2048]{1,0:T(8,128)S(1)}) custom-call(bf16[4,128,768]{2,1,0:T(8,128)(2,1)S(1)} %all_to_all.26.r3_ref, bf16[2048,1024]{1,0:T(8,128)(2,1)S(1)} %copy-done, bf16[128,256]{1,0:T(8,128)(2,1)S(1)} %copy-done.8, f32[128,16]{1,0:T(8,128)S(1)} %copy.16.dt_ref, f32[1,16]{1,0:T(1,128)S(1)} %bitcast.5), custom_call_target="tpu_custom_call" | custom-call | flops 1073741824 | bytes 8388608 | tf_op jit(solution)/shard_map/value_back/pallas_call | solution.py:369
  122.1 28.2 %all_to_all.27.r4_ref = bf16[32,192,128]{2,1,0:T(8,128)(2,1)} all-to-all(bf16[32,192,128]{2,1,0:T(8,128)(2,1)S(1)} %get-tuple-element.22), channel_id=1, replica_groups=mesh['ctx'=32,'ch'=2,'section'=2] {'ctx'}, dimensions={0} | all-to-all | bytes 3145728 | tf_op jit(solution)/shard_map/all_to_all | solution.py:384
  150.3 16.8 %attention_grads.1 = (bf16[32,192,128]{2,1,0:T(8,128)(2,1)}, f32[256,1024]{1,0:T(8,128)}, bf16[256,1024]{1,0:T(8,128)(2,1)}) custom-call(s32[1]{0:T(128)} %bitcast.at_ref, bf16[32,208,128]{2,1,0:T(8,128)(2,1)} %copy-done.3, bf16[32,192,128]{2,1,0:T(8,128)(2,1)} %all_to_all.27.r4_ref, bf16[2,1024,128]{2,1,0:T(8,128)(2,1)} %copy-done.9, ...), custom_call_target="tpu_custom_call" | custom-call | flops 4294967296 | bytes 33554432 | tf_op jit(solution)/shard_map/attention_grads/pallas_call | solution.py:369
  167.1 4.7 %all-to-all-start.4 = ((bf16[32,192,128]{2,1,0:T(8,128)(2,1)}), bf16[32,192,128]{2,1,0:T(8,128)(2,1)}, u32[]{:S(2)}, u32[]{:S(2)}) async-start(bf16[32,192,128]{2,1,0:T(8,128)(2,1)} %get-tuple-element.31), calls=%async_computation.4 | async-start | bytes 3145728 | tf_op jit(solution)/shard_map/all_to_all | solution.py:384
  171.9 7.8 %collective-permute-start.1 = (bf16[256,1024]{1,0:T(8,128)(2,1)}, bf16[256,1024]{1,0:T(8,128)(2,1)S(1)}, u32[]{:S(2)}, u32[]{:S(2)}) collective-permute-start(bf16[256,1024]{1,0:T(8,128)(2,1)} %get-tuple-element.26), channel_id=1, source_target_pairs={{0,124},{4,120},{8,116},{12,112},{16,108},{20,104},{24,100},{28,96... | collective-permute-start | bytes 1572872 | tf_op jit(solution)/shard_map/ppermute | solution.py:448
  179.7 1.2 copy-done.7
  180.9 2.5 %mixer_local.1 = (f32[128,2048]{1,0:T(8,128)S(1)}, f32[128,256]{1,0:T(8,128)S(1)}, f32[128,256]{1,0:T(8,128)}) custom-call(bf16[128,2048]{1,0:T(8,128)(2,1)S(1)} %copy-done.2, bf16[128,256]{1,0:T(8,128)(2,1)S(1)} %copy-done.5, bf16[128,256]{1,0:T(8,128)(2,1)S(1)} %copy-done.8, f32[128,16]{1,0:T(8,128)S(1)} %copy.16.dt_ref, f32[1,16]{1,0:T(1,128)S(1)} %bitcast.6, ...), custom_call_target="tpu_custom_call" | custom-call | flops 536870912 | bytes 8388608 | tf_op jit(solution)/shard_map/mixer_local/pallas_call | solution.py:369
  183.4 23.5 %collective-permute-done.1 = bf16[256,1024]{1,0:T(8,128)(2,1)S(1)} collective-permute-done((bf16[256,1024]{1,0:T(8,128)(2,1)}, bf16[256,1024]{1,0:T(8,128)(2,1)S(1)}, u32[]{:S(2)}, u32[]{:S(2)}) %collective-permute-start.1) | collective-permute-done | bytes 524320 | tf_op jit(solution)/shard_map/ppermute | solution.py:448
  206.9 0.1 convert_element_type.3
  207.0 0.3 maximum_select_fusion
  207.4 1.5 fusion
  208.8 3.2 %mixer_grads.1 = (f32[128,2048]{1,0:T(8,128)}, f32[128,256]{1,0:T(8,128)}, f32[128,256]{1,0:T(8,128)}) custom-call(bf16[128,2048]{1,0:T(8,128)(2,1)S(1)} %copy-done.2, bf16[128,256]{1,0:T(8,128)(2,1)S(1)} %copy-done.5, f32[128,16]{1,0:T(8,128)S(1)} %copy.16.dt_ref, f32[1,16]{1,0:T(1,128)S(1)} %bitcast.7, f32[128,2048]{1,0:T(8,128)S(1)} %get-tuple-element.29.gx0_ref, ...), custom_call_target="tpu_custom_call" | custom-call | flops 536870912 | bytes 8388608 | tf_op jit(solution)/shard_map/mixer_grads/pallas_call | solution.py:369
  (32 shorter events, 0.1 us)
Async XLA Ops:
  1.4 1.0 copy-start.1
  2.5 0.8 copy-start.4
  3.3 0.8 copy-start.13
  4.2 0.7 copy-start.14
  7.2 10.9 %copy-start.11 = (bf16[128,2048]{1,0:T(8,128)(2,1)S(1)}, bf16[128,2048]{1,0:T(8,128)(2,1)}, u32[]{:S(2)}) copy-start(bf16[128,2048]{1,0:T(8,128)(2,1)} %q_ref.1) | copy-start | bytes 1572868
  7.2 10.9 %copy-start.12 = (bf16[128,2048]{1,0:T(8,128)(2,1)S(1)}, bf16[128,2048]{1,0:T(8,128)(2,1)}, u32[]{:S(2)}) copy-start(bf16[128,2048]{1,0:T(8,128)(2,1)} %d_ref.1) | copy-start | bytes 1572868
  7.2 49.0 %all-to-all-start = ((bf16[32,208,128]{2,1,0:T(8,128)(2,1)}), bf16[32,208,128]{2,1,0:T(8,128)(2,1)S(1)}, u32[]{:S(2)}, u32[]{:S(2)}) async-start(bf16[32,208,128]{2,1,0:T(8,128)(2,1)} %block_states.1), calls=%async_computation | async-start | bytes 3407872 | tf_op jit(solution)/shard_map/all_to_all | solution.py:384
  18.2 37.2 %collective-permute-start = (bf16[256,1024]{1,0:T(8,128)(2,1)S(1)}, bf16[256,1024]{1,0:T(8,128)(2,1)S(1)}, u32[]{:S(2)}, u32[]{:S(2)}) collective-permute-start(bf16[256,1024]{1,0:T(8,128)(2,1)S(1)} %pad_maximum_fusion), channel_id=1, source_target_pairs={{0,124},{4,120},{8,116},{12,112},{16,108},{20,104},{24,100},{28,96... | collective-permute-start | bytes 1572872 | tf_op jit(solution)/shard_map/ppermute | solution.py:404
  55.3 0.8 copy-start.17
  56.1 1.0 copy-start.18
  57.2 43.2 %copy-start = (bf16[2048,1024]{1,0:T(8,128)(2,1)S(1)}, bf16[2048,1024]{1,0:T(8,128)(2,1)}, u32[]{:S(2)}) copy-start(bf16[2048,1024]{1,0:T(8,128)(2,1)} %w_ref.3) | copy-start | bytes 12582916
  71.3 1.2 copy-start.3
  72.5 30.1 %copy-start.9 = (bf16[2,1024,128]{2,1,0:T(8,128)(2,1)}, bf16[2,1024,128]{2,1,0:T(8,128)(2,1)S(1)}, u32[]{:S(2)}) copy-start(bf16[2,1024,128]{2,1,0:T(8,128)(2,1)S(1)} %get-tuple-element.23.qs_ref) | copy-start | bytes 1572868
  72.5 30.1 %copy-start.10 = (bf16[2,1024,128]{2,1,0:T(8,128)(2,1)}, bf16[2,1024,128]{2,1,0:T(8,128)(2,1)S(1)}, u32[]{:S(2)}) copy-start(bf16[2,1024,128]{2,1,0:T(8,128)(2,1)S(1)} %get-tuple-element.24.ds_ref) | copy-start | bytes 1572868
  72.5 27.9 %copy-start.2 = (bf16[128,2048]{1,0:T(8,128)(2,1)S(1)}, bf16[128,2048]{1,0:T(8,128)(2,1)}, u32[]{:S(2)}) copy-start(bf16[128,2048]{1,0:T(8,128)(2,1)} %x_ref.7) | copy-start | bytes 1572868
  72.5 27.9 %copy-start.5 = (bf16[128,256]{1,0:T(8,128)(2,1)S(1)}, bf16[128,256]{1,0:T(8,128)(2,1)}, u32[]{:S(2)}) copy-start(bf16[128,256]{1,0:T(8,128)(2,1)} %b_ref.7) | copy-start | bytes 196612
  72.5 27.9 %copy-start.8 = (bf16[128,256]{1,0:T(8,128)(2,1)S(1)}, bf16[128,256]{1,0:T(8,128)(2,1)}, u32[]{:S(2)}) copy-start(bf16[128,256]{1,0:T(8,128)(2,1)} %c_ref.5) | copy-start | bytes 196612
  72.5 27.9 %copy-start.15 = (f32[16]{0:T(128)S(1)}, f32[16]{0:T(128)}, u32[]{:S(2)}) copy-start(f32[16]{0:T(128)} %param.14) | copy-start | bytes 196
  72.6 27.9 %copy-start.16 = (f32[16]{0:T(128)S(1)}, f32[16]{0:T(128)}, u32[]{:S(2)}) copy-start(f32[16]{0:T(128)} %param.15) | copy-start | bytes 196
  122.1 28.2 %copy-start.6 = (f32[128,2048]{1,0:T(8,128)}, f32[128,2048]{1,0:T(8,128)S(1)}, u32[]{:S(2)}) copy-start(f32[128,2048]{1,0:T(8,128)S(1)} %get-tuple-element.28.dy_ref) | copy-start | bytes 3145732
  167.1 41.7 %all-to-all-start.4 = ((bf16[32,192,128]{2,1,0:T(8,128)(2,1)}), bf16[32,192,128]{2,1,0:T(8,128)(2,1)}, u32[]{:S(2)}, u32[]{:S(2)}) async-start(bf16[32,192,128]{2,1,0:T(8,128)(2,1)} %get-tuple-element.31), calls=%async_computation.4 | async-start | bytes 3145728 | tf_op jit(solution)/shard_map/all_to_all | solution.py:384
  171.9 35.0 %collective-permute-start.1 = (bf16[256,1024]{1,0:T(8,128)(2,1)}, bf16[256,1024]{1,0:T(8,128)(2,1)S(1)}, u32[]{:S(2)}, u32[]{:S(2)}) collective-permute-start(bf16[256,1024]{1,0:T(8,128)(2,1)} %get-tuple-element.26), channel_id=1, source_target_pairs={{0,124},{4,120},{8,116},{12,112},{16,108},{20,104},{24,100},{28,96... | collective-permute-start | bytes 1572872 | tf_op jit(solution)/shard_map/ppermute | solution.py:448
  179.7 1.2 copy-start.7
  180.9 26.1 %copy-start.19 = (f32[256,1024]{1,0:T(8,128)S(1)}, f32[256,1024]{1,0:T(8,128)}, u32[]{:S(2)}) copy-start(f32[256,1024]{1,0:T(8,128)} %get-tuple-element.27) | copy-start | bytes 3145732

commit v3 on v2

--- a/solution.py
+++ b/solution.py
@@ -213,29 +213,29 @@
             acc = acc + r2_ref[16 * k + s, SR : SR + T, :].astype(F32)
         dv.append(acc.astype(BF))
     for d in range(4):
-        big, rest = split(mm(y_sc[...], w_ref[:, quarter(d)]))
-        out_ref[d, :, 0:256] = big
-        out_ref[d, :, 256:512] = rest
-        out_ref[d, :, 512:640] = dv[0]
-        out_ref[d, :, 640:768] = dv[1]
+        out_ref[d, :, 0:256] = mm(y_sc[...], w_ref[:, quarter(d)]).astype(BF)
+        out_ref[d, :, 256:384] = dv[0]
+        out_ref[d, :, 384:512] = dv[1]
 
 
 def back_kernel(r3_ref, w_ref, c_ref, dt_ref, a_ref, pay_ref, dy_ref):
-    values = r3_ref[0, :, 0:256].astype(F32) + r3_ref[0, :, 256:512].astype(F32)
+    values = r3_ref[0, :, 0:256].astype(F32)
     for s in range(1, 4):
         values = values + r3_ref[s, :, 0:256].astype(F32)
-        values = values + r3_ref[s, :, 256:512].astype(F32)
     values = values.astype(BF)
     for d in range(32):
         pay_ref[d, SR : SR + T, :] = values[:, head(d // 16)]
-    vg = jnp.concatenate([r3_ref[s, :, 512:768] for s in range(4)], axis=1)
+    vg = jnp.concatenate([r3_ref[s, :, 256:512] for s in range(4)], axis=1)
     grow = jnp.exp(sums_by_token(dt_ref, a_ref))
-    for h in range(NH):
-        dy = mm(vg, w_ref[head(h), :], NT)
-        dy_ref[:, head(h)] = dy
-        eg = mm((dy * grow[:, h : h + 1]).astype(BF), c_ref[:, head(h // GH)], TN).astype(BF)
-        pay_ref[2 * h, 0:SR, :] = eg[0:SR]
-        pay_ref[2 * h + 1, 0:SR, :] = eg[SR:T]
+    for pair in range(NH // 2):
+        both = mm(vg, w_ref[quarter(pair), :], NT)
+        dy_ref[:, quarter(pair)] = both
+        for n in range(2):
+            h = 2 * pair + n
+            grown = (both[:, head(n)] * grow[:, h : h + 1]).astype(BF)
+            eg = mm(grown, c_ref[:, head(h // GH)], TN).astype(BF)
+            pay_ref[2 * h, 0:SR, :] = eg[0:SR]
+            pay_ref[2 * h + 1, 0:SR, :] = eg[SR:T]
 
 
 def grads_kernel(
@@ -403,7 +403,7 @@
     )
     other = lax.ppermute(away, "ctx", swap)
     (pay1,) = call(
-        state_kernel, [((32, SR + DR + T, T), BF)], [], "block_states", 24, 1 << 27, 1 << 22,
+        state_kernel, [((32, SR + DR + T, T), BF)], [], "block_states", 62, 1 << 34, 1 << 22,
         mamba_x, mamba_b, step_dt, a_row, keys,
     )
     r1 = over_ctx(pay1)
@@ -418,7 +418,7 @@
     )
     r2 = over_ctx(pay2)
     (pay3,) = call(
-        values_kernel, [((4, T, 768), BF)], [pltpu.VMEM((T, 2048), BF)], "values", 24,
+        values_kernel, [((4, T, 512), BF)], [pltpu.VMEM((T, 2048), BF)], "values", 24,
         1 << 30, 1 << 23,
         mamba_x, mamba_b, mamba_c, step_dt, a_row, skip_row, r2, value_weight,
     )

time: 213 us -> 205 us (0.962)
  local copies, waits for them, and re-layouts: 9.97 us -> 6.46 us
    unnamed x41 -> x39, local copies, waits for them, and re-layouts: 8.51 us -> 5 us
    all_to_all x1, blocking collectives: 14.1 us -> 11.2 us  [body(): r3 = lax.all_to_all(pay3, ('ch', 'section'), 0, 0, tiled=True)]
where the time goes in v3:
time: 205 us; the launch traced here: 204 us
  blocking collectives  68.2 us (33%)
  waiting for transfers between devices  52.4 us (26%)
  Pallas kernels  44.8 us (22%)
  starting transfers between devices  30.6 us (15%)
  local copies, waits for them, and re-layouts  6.46 us (3%)
    all_to_all x2, blocking collectives, over_ctx(): return lax.all_to_all(pay, 'ctx', 0, 0, tiled=True)  57 us
    pallas_call x7, Pallas kernels, call(): pl.pallas_call(kernel, name=name, out_shape=[jax.ShapeDtypeStruct(s, d) f...  44.8 us
    ppermute x1, waiting for transfers between devices, body(): other = lax.ppermute(away, 'ctx', swap)  29.5 us
    ppermute x1, waiting for transfers between devices, body(): back = lax.ppermute(send, 'ctx', swap)  22.9 us
    all_to_all x2, starting transfers between devices, over_ctx(): return lax.all_to_all(pay, 'ctx', 0, 0, tiled=True)  15.2 us
    all_to_all x1, blocking collectives, body(): r3 = lax.all_to_all(pay3, ('ch', 'section'), 0, 0, tiled=True)  11.2 us
    ppermute x1, starting transfers between devices, body(): other = lax.ppermute(away, 'ctx', swap)  7.68 us
    ppermute x1, starting transfers between devices, body(): back = lax.ppermute(send, 'ctx', swap)  7.68 us
  transfers between devices with their start and end apart: 4, of which 2 were waited for; matrix products, arithmetic and copies ran while one was open for 1% of the time, Pallas kernels for 1%

profile of v3, /device:TPU:0, one launch (start us, length us, event | category | flops | bytes accessed | tf_op | source)
XLA Modules:
  0.0 203.9 jit_solution(6792359682871761801)
XLA Ops:
  0.6 1.4 copy.16.dt_ref
  2.1 3.5 %block_states.1 = bf16[32,208,128]{2,1,0:T(8,128)(2,1)} custom-call(bf16[128,2048]{1,0:T(8,128)(2,1)} %x_ref.7, bf16[128,256]{1,0:T(8,128)(2,1)} %b_ref.7, f32[128,16]{1,0:T(8,128)} %copy.16.dt_ref, f32[1,16]{1,0:T(1,128)} %bitcast.3, bf16[128,256]{1,0:T(8,128)(2,1)} %k_ref.1), custom_call_target="tpu_custom_call" | custom-call | flops 17179869184 | bytes 4194304 | tf_op jit(solution)/shard_map/block_states/pallas_call | solution.py:369
  5.5 10.8 %all-to-all-start = ((bf16[32,208,128]{2,1,0:T(8,128)(2,1)}), bf16[32,208,128]{2,1,0:T(8,128)(2,1)S(1)}, u32[]{:S(2)}, u32[]{:S(2)}) async-start(bf16[32,208,128]{2,1,0:T(8,128)(2,1)} %block_states.1), calls=%async_computation | async-start | bytes 3407872 | tf_op jit(solution)/shard_map/all_to_all | solution.py:384
  16.4 0.1 slice_select_fusion
  16.5 7.7 %collective-permute-start = (bf16[256,1024]{1,0:T(8,128)(2,1)S(1)}, bf16[256,1024]{1,0:T(8,128)(2,1)S(1)}, u32[]{:S(2)}, u32[]{:S(2)}) collective-permute-start(bf16[256,1024]{1,0:T(8,128)(2,1)S(1)} %pad_maximum_fusion), channel_id=1, source_target_pairs={{0,124},{4,120},{8,116},{12,112},{16,108},{20,104},{24,100},{28,96... | collective-permute-start | bytes 1572872 | tf_op jit(solution)/shard_map/ppermute | solution.py:404
  24.2 29.5 %collective-permute-done.other_ref = bf16[256,1024]{1,0:T(8,128)(2,1)S(1)} collective-permute-done((bf16[256,1024]{1,0:T(8,128)(2,1)S(1)}, bf16[256,1024]{1,0:T(8,128)(2,1)S(1)}, u32[]{:S(2)}, u32[]{:S(2)}) %collective-permute-start) | collective-permute-done | bytes 524320 | tf_op jit(solution)/shard_map/ppermute | solution.py:404
  53.7 14.1 %probs.1 = (bf16[32,192,128]{2,1,0:T(8,128)(2,1)S(1)}, f32[33,128,1024]{2,1,0:T(8,128)}, bf16[2,1024,128]{2,1,0:T(8,128)(2,1)S(1)}, bf16[2,1024,128]{2,1,0:T(8,128)(2,1)S(1)}) custom-call(s32[1]{0:T(128)} %bitcast.at_ref, bf16[32,208,128]{2,1,0:T(8,128)(2,1)S(1)} %all-to-all-done.r1_ref, bf16[128,2048]{1,0:T(8,128)(2,1)S(1)} %copy-done.14, ...), custom_call_target="tpu_custom_call" | custom-call | flops 4294967296 | bytes 33554432 | tf_op jit(solution)/shard_map/probs/pallas_call | solution.py:369
  67.8 0.0 copy-start.12
  67.9 0.0 copy-start.2
  67.9 0.0 copy-start.5
  67.9 0.0 copy-start.10
  67.9 0.0 copy-start.11
  67.9 0.0 copy-start.16
  67.9 0.0 copy-start.17
  67.9 28.7 %all_to_all.25.r2_ref = bf16[32,192,128]{2,1,0:T(8,128)(2,1)S(1)} all-to-all(bf16[32,192,128]{2,1,0:T(8,128)(2,1)S(1)} %get-tuple-element.21), channel_id=1, replica_groups=mesh['ctx'=32,'ch'=2,'section'=2] {'ctx'}, dimensions={0} | all-to-all | bytes 3145728 | tf_op jit(solution)/shard_map/all_to_all | solution.py:384
  96.7 2.1 %values.1 = bf16[4,128,512]{2,1,0:T(8,128)(2,1)S(1)} custom-call(bf16[128,2048]{1,0:T(8,128)(2,1)S(1)} %copy-done.2, bf16[128,256]{1,0:T(8,128)(2,1)S(1)} %copy-done.11, bf16[128,256]{1,0:T(8,128)(2,1)S(1)} %copy-done.10, f32[128,16]{1,0:T(8,128)S(1)} %copy-done.5, f32[1,16]{1,0:T(1,128)S(1)} %bitcast.4, f32[1,16]{1,0:T(1,128)S(1)} %bitcast.8, ...), custom_call_target="tpu_custom_call" | custom-call | flops 1073741824 | bytes 8388608 | tf_op jit(solution)/shard_map/values/pallas_call | solution.py:369
  98.9 11.2 %all_to_all.26.r3_ref = bf16[4,128,512]{2,1,0:T(8,128)(2,1)S(1)} all-to-all(bf16[4,128,512]{2,1,0:T(8,128)(2,1)S(1)} %values.1), channel_id=1, replica_groups=mesh['ctx'=32,'ch'=2,'section'=2] {'ch','section'}, dimensions={0} | all-to-all | bytes 1048576 | tf_op jit(solution)/shard_map/all_to_all | solution.py:425
  110.1 4.0 %value_back.1 = (bf16[32,192,128]{2,1,0:T(8,128)(2,1)S(1)}, f32[128,2048]{1,0:T(8,128)S(1)}) custom-call(bf16[4,128,512]{2,1,0:T(8,128)(2,1)S(1)} %all_to_all.26.r3_ref, bf16[2048,1024]{1,0:T(8,128)(2,1)S(1)} %copy-done, bf16[128,256]{1,0:T(8,128)(2,1)S(1)} %copy-done.10, f32[128,16]{1,0:T(8,128)S(1)} %copy-done.5, f32[1,16]{1,0:T(1,128)S(1)} %bitcast.5), custom_call_target="tpu_custom_call" | custom-call | flops 1073741824 | bytes 8388608 | tf_op jit(solution)/shard_map/value_back/pallas_call | solution.py:369
  114.1 0.0 copy-start.8
  114.1 28.2 %all_to_all.27.r4_ref = bf16[32,192,128]{2,1,0:T(8,128)(2,1)} all-to-all(bf16[32,192,128]{2,1,0:T(8,128)(2,1)S(1)} %get-tuple-element.22), channel_id=1, replica_groups=mesh['ctx'=32,'ch'=2,'section'=2] {'ctx'}, dimensions={0} | all-to-all | bytes 3145728 | tf_op jit(solution)/shard_map/all_to_all | solution.py:384
  142.4 16.8 %attention_grads.1 = (bf16[32,192,128]{2,1,0:T(8,128)(2,1)}, f32[256,1024]{1,0:T(8,128)}, bf16[256,1024]{1,0:T(8,128)(2,1)}) custom-call(s32[1]{0:T(128)} %bitcast.at_ref, bf16[32,208,128]{2,1,0:T(8,128)(2,1)} %copy-done.1, bf16[32,192,128]{2,1,0:T(8,128)(2,1)} %all_to_all.27.r4_ref, bf16[2,1024,128]{2,1,0:T(8,128)(2,1)} %copy-done.12, ...), custom_call_target="tpu_custom_call" | custom-call | flops 4294967296 | bytes 33554432 | tf_op jit(solution)/shard_map/attention_grads/pallas_call | solution.py:369
  159.2 4.4 %all-to-all-start.4 = ((bf16[32,192,128]{2,1,0:T(8,128)(2,1)}), bf16[32,192,128]{2,1,0:T(8,128)(2,1)S(1)}, u32[]{:S(2)}, u32[]{:S(2)}) async-start(bf16[32,192,128]{2,1,0:T(8,128)(2,1)} %get-tuple-element.31), calls=%async_computation.4 | async-start | bytes 3145728 | tf_op jit(solution)/shard_map/all_to_all | solution.py:384
  163.6 7.7 %collective-permute-start.1 = (bf16[256,1024]{1,0:T(8,128)(2,1)}, bf16[256,1024]{1,0:T(8,128)(2,1)S(1)}, u32[]{:S(2)}, u32[]{:S(2)}) collective-permute-start(bf16[256,1024]{1,0:T(8,128)(2,1)} %get-tuple-element.26), channel_id=1, source_target_pairs={{0,124},{4,120},{8,116},{12,112},{16,108},{20,104},{24,100},{28,96... | collective-permute-start | bytes 1572872 | tf_op jit(solution)/shard_map/ppermute | solution.py:448
  171.3 1.0 copy-done.3
  172.4 1.2 copy-done.9
  173.6 2.5 %mixer_local.1 = (f32[128,2048]{1,0:T(8,128)S(1)}, f32[128,256]{1,0:T(8,128)S(1)}, f32[128,256]{1,0:T(8,128)}) custom-call(bf16[128,2048]{1,0:T(8,128)(2,1)S(1)} %copy-done.3, bf16[128,256]{1,0:T(8,128)(2,1)S(1)} %copy-done.11, bf16[128,256]{1,0:T(8,128)(2,1)S(1)} %copy-done.10, f32[128,16]{1,0:T(8,128)S(1)} %copy-done.5, f32[1,16]{1,0:T(1,128)S(1)} %bitcast.6, ...), custom_call_target="tpu_custom_call" | custom-call | flops 536870912 | bytes 8388608 | tf_op jit(solution)/shard_map/mixer_local/pallas_call | solution.py:369
  176.1 22.9 %collective-permute-done.1 = bf16[256,1024]{1,0:T(8,128)(2,1)S(1)} collective-permute-done((bf16[256,1024]{1,0:T(8,128)(2,1)}, bf16[256,1024]{1,0:T(8,128)(2,1)S(1)}, u32[]{:S(2)}, u32[]{:S(2)}) %collective-permute-start.1) | collective-permute-done | bytes 524320 | tf_op jit(solution)/shard_map/ppermute | solution.py:448
  199.0 0.1 convert_element_type.3
  199.1 0.3 maximum_select_fusion
  199.5 1.5 fusion
  201.0 1.2 copy-done.7
  202.2 1.8 mixer_grads.1
  (30 shorter events, 0.1 us)
Async XLA Ops:
  5.5 10.9 %copy-start.14 = (bf16[128,2048]{1,0:T(8,128)(2,1)S(1)}, bf16[128,2048]{1,0:T(8,128)(2,1)}, u32[]{:S(2)}) copy-start(bf16[128,2048]{1,0:T(8,128)(2,1)} %q_ref.1) | copy-start | bytes 1572868
  5.5 10.9 %copy-start.15 = (bf16[128,2048]{1,0:T(8,128)(2,1)S(1)}, bf16[128,2048]{1,0:T(8,128)(2,1)}, u32[]{:S(2)}) copy-start(bf16[128,2048]{1,0:T(8,128)(2,1)} %d_ref.1) | copy-start | bytes 1572868
  5.5 48.2 %all-to-all-start = ((bf16[32,208,128]{2,1,0:T(8,128)(2,1)}), bf16[32,208,128]{2,1,0:T(8,128)(2,1)S(1)}, u32[]{:S(2)}, u32[]{:S(2)}) async-start(bf16[32,208,128]{2,1,0:T(8,128)(2,1)} %block_states.1), calls=%async_computation | async-start | bytes 3407872 | tf_op jit(solution)/shard_map/all_to_all | solution.py:384
  16.5 37.2 %collective-permute-start = (bf16[256,1024]{1,0:T(8,128)(2,1)S(1)}, bf16[256,1024]{1,0:T(8,128)(2,1)S(1)}, u32[]{:S(2)}, u32[]{:S(2)}) collective-permute-start(bf16[256,1024]{1,0:T(8,128)(2,1)S(1)} %pad_maximum_fusion), channel_id=1, source_target_pairs={{0,124},{4,120},{8,116},{12,112},{16,108},{20,104},{24,100},{28,96... | collective-permute-start | bytes 1572872 | tf_op jit(solution)/shard_map/ppermute | solution.py:404
  53.7 14.1 %copy-start.1 = (bf16[32,208,128]{2,1,0:T(8,128)(2,1)}, bf16[32,208,128]{2,1,0:T(8,128)(2,1)S(1)}, u32[]{:S(2)}) copy-start(bf16[32,208,128]{2,1,0:T(8,128)(2,1)S(1)} %all-to-all-done.r1_ref) | copy-start | bytes 5111812
  53.7 43.0 %copy-start = (bf16[2048,1024]{1,0:T(8,128)(2,1)S(1)}, bf16[2048,1024]{1,0:T(8,128)(2,1)}, u32[]{:S(2)}) copy-start(bf16[2048,1024]{1,0:T(8,128)(2,1)} %w_ref.3) | copy-start | bytes 12582916
  67.8 31.0 %copy-start.12 = (bf16[2,1024,128]{2,1,0:T(8,128)(2,1)}, bf16[2,1024,128]{2,1,0:T(8,128)(2,1)S(1)}, u32[]{:S(2)}) copy-start(bf16[2,1024,128]{2,1,0:T(8,128)(2,1)S(1)} %get-tuple-element.23.qs_ref) | copy-start | bytes 1572868
  67.9 31.0 %copy-start.13 = (bf16[2,1024,128]{2,1,0:T(8,128)(2,1)}, bf16[2,1024,128]{2,1,0:T(8,128)(2,1)S(1)}, u32[]{:S(2)}) copy-start(bf16[2,1024,128]{2,1,0:T(8,128)(2,1)S(1)} %get-tuple-element.24.ds_ref) | copy-start | bytes 1572868
  67.9 28.8 %copy-start.2 = (bf16[128,2048]{1,0:T(8,128)(2,1)S(1)}, bf16[128,2048]{1,0:T(8,128)(2,1)}, u32[]{:S(2)}) copy-start(bf16[128,2048]{1,0:T(8,128)(2,1)} %x_ref.7) | copy-start | bytes 1572868
  67.9 28.8 %copy-start.5 = (f32[128,16]{1,0:T(8,128)S(1)}, f32[128,16]{1,0:T(8,128)}, u32[]{:S(2)}) copy-start(f32[128,16]{1,0:T(8,128)} %copy.16.dt_ref) | copy-start | bytes 24580
  67.9 28.8 %copy-start.10 = (bf16[128,256]{1,0:T(8,128)(2,1)S(1)}, bf16[128,256]{1,0:T(8,128)(2,1)}, u32[]{:S(2)}) copy-start(bf16[128,256]{1,0:T(8,128)(2,1)} %c_ref.5) | copy-start | bytes 196612
  67.9 28.8 %copy-start.11 = (bf16[128,256]{1,0:T(8,128)(2,1)S(1)}, bf16[128,256]{1,0:T(8,128)(2,1)}, u32[]{:S(2)}) copy-start(bf16[128,256]{1,0:T(8,128)(2,1)} %b_ref.7) | copy-start | bytes 196612
  67.9 28.8 %copy-start.16 = (f32[16]{0:T(128)S(1)}, f32[16]{0:T(128)}, u32[]{:S(2)}) copy-start(f32[16]{0:T(128)} %param.14) | copy-start | bytes 196
  67.9 28.8 %copy-start.17 = (f32[16]{0:T(128)S(1)}, f32[16]{0:T(128)}, u32[]{:S(2)}) copy-start(f32[16]{0:T(128)} %param.15) | copy-start | bytes 196
  114.1 28.3 %copy-start.8 = (f32[128,2048]{1,0:T(8,128)}, f32[128,2048]{1,0:T(8,128)S(1)}, u32[]{:S(2)}) copy-start(f32[128,2048]{1,0:T(8,128)S(1)} %get-tuple-element.28.dy_ref) | copy-start | bytes 3145732
  159.2 41.7 %all-to-all-start.4 = ((bf16[32,192,128]{2,1,0:T(8,128)(2,1)}), bf16[32,192,128]{2,1,0:T(8,128)(2,1)S(1)}, u32[]{:S(2)}, u32[]{:S(2)}) async-start(bf16[32,192,128]{2,1,0:T(8,128)(2,1)} %get-tuple-element.31), calls=%async_computation.4 | async-start | bytes 3145728 | tf_op jit(solution)/shard_map/all_to_all | solution.py:384
  163.6 35.3 %collective-permute-start.1 = (bf16[256,1024]{1,0:T(8,128)(2,1)}, bf16[256,1024]{1,0:T(8,128)(2,1)S(1)}, u32[]{:S(2)}, u32[]{:S(2)}) collective-permute-start(bf16[256,1024]{1,0:T(8,128)(2,1)} %get-tuple-element.26), channel_id=1, source_target_pairs={{0,124},{4,120},{8,116},{12,112},{16,108},{20,104},{24,100},{28,96... | collective-permute-start | bytes 1572872 | tf_op jit(solution)/shard_map/ppermute | solution.py:448
  171.3 1.0 copy-start.3
  172.4 1.2 copy-start.9
  173.6 25.5 %copy-start.18 = (f32[256,1024]{1,0:T(8,128)S(1)}, f32[256,1024]{1,0:T(8,128)}, u32[]{:S(2)}) copy-start(f32[256,1024]{1,0:T(8,128)} %get-tuple-element.27) | copy-start | bytes 3145732
  176.1 23.4 %copy-start.6 = (f32[128,2048]{1,0:T(8,128)}, f32[128,2048]{1,0:T(8,128)S(1)}, u32[]{:S(2)}) copy-start(f32[128,2048]{1,0:T(8,128)S(1)} %get-tuple-element.29.gx0_ref) | copy-start | bytes 3145732
  199.5 1.5 copy-start.4
  200.9 1.2 copy-start.7

commit v4 on v3

--- a/solution.py
+++ b/solution.py
@@ -17,6 +17,7 @@
 SR = 64
 DR = 16
 NEG = -1e30
+NB = 40
 
 NN = (((1,), (0,)), ((), ()))
 NT = (((1,), (1,)), ((), ()))
@@ -41,24 +42,28 @@
     return row >= col
 
 
-def sums_by_token(dt_ref, a_ref):
-    steps = -dt_ref[...] * a_ref[...]
-    return mm_exact(lower_tri().astype(F32), steps)
-
-
-def sums_by_head(dt_ref, a_ref):
+def same_token():
     row = lax.broadcasted_iota(jnp.int32, (T, T), 0)
     col = lax.broadcasted_iota(jnp.int32, (T, T), 1)
-    steps = -dt_ref[...] * a_ref[...]
-    upper = (row <= col).astype(F32)
-    same = (row == col).astype(F32)
-    return mm_exact(steps, upper, TN), mm_exact(dt_ref[...], same, TN)
+    return (row == col).astype(F32)
+
+
+def sums_by_token(dt_ref, a_ref):
+    return -mm_exact(lower_tri().astype(F32), dt_ref[...], NT) * a_ref[...]
+
+
+def steps_by_token(dt_ref):
+    return mm_exact(same_token(), dt_ref[...], NT)
+
+
+def sums_by_head(cum):
+    return mm_exact(cum, same_token(), TN)
 
 
 def state_kernel(x_ref, b_ref, dt_ref, a_ref, k_ref, out_ref):
     cum = sums_by_token(dt_ref, a_ref)
     total = cum[T - 1 : T, :]
-    weight = jnp.exp(total - cum) * dt_ref[...]
+    weight = jnp.exp(total - cum) * steps_by_token(dt_ref)
     first = total.astype(BF).astype(F32)
     second = (total - first).astype(BF).astype(F32)
     third = total - first - second
@@ -80,17 +85,24 @@
         out_ref[d, SR + DR : SR + DR + T, :] = k_ref[:, head(d // 16)]
 
 
+def partner_of(at):
+    return at + 24 - 16 * (at // 8)
+
+
 def decay_of(r1_ref, c):
     parts = r1_ref[c, SR : SR + DR, :].astype(F32)
     return jnp.exp(parts[0:1] + parts[1:2] + parts[2:3])
 
 
 def steps_of(n, step, init):
-    whole = n // 4
-    init = lax.fori_loop(0, whole, lambda i, c: step(i * 4, 4, c), init)
-    pairs = (n - whole * 4) // 2
-    init = lax.fori_loop(0, pairs, lambda i, c: step(whole * 4, 2, c), init)
-    return lax.fori_loop(whole * 4 + pairs * 2, n, lambda i, c: step(i, 1, c), init)
+    at = 0
+    for size in (8, 4, 2, 1):
+        whole = (n - at) // size
+        init = lax.fori_loop(
+            0, whole, lambda i, c, at=at, size=size: step(at + i * size, size, c), init
+        )
+        at = at + whole * size
+    return init
 
 
 def rows_of(ref, j, u, first):
@@ -111,7 +123,8 @@
 ):
     at = at_ref[0]
     upper = (at >= 16).astype(jnp.int32)
-    low = jnp.minimum(at, 31 - at)
+    low = jnp.minimum(at, partner_of(at))
+    high = jnp.maximum(at, partner_of(at))
 
     for h in range(GH):
         own = pl.ds(pl.multiple_of(upper * 1024 + h * T, T), T)
@@ -128,7 +141,7 @@
     seen = key <= tok
 
     for sel in range(2):
-        count = low if sel == 0 else 31 - low
+        count = low if sel == 0 else high
         base = 0 if sel == 0 else low + 1
 
         def scores(j, u, top, diag=False, sel=sel, base=base):
@@ -180,7 +193,12 @@
         run = decay_of(r1_ref, c) * run + r1_ref[c, 0:SR, :].astype(F32)
     for c in range(32):
         pay_ref[c, SR : SR + T, :] = dv_sc[c].astype(BF)
-    pltpu.make_async_copy(s_sc, p_hbm, sem).wait()
+
+    def finish(b, none):
+        pltpu.make_async_copy(s_sc.at[b], p_hbm.at[b], sem).wait()
+        return none
+
+    lax.fori_loop(0, low + high + 2, finish, 0)
 
 
 def split(x):
@@ -192,7 +210,7 @@
     x_ref, b_ref, c_ref, dt_ref, a_ref, skip_ref, r2_ref, w_ref, out_ref, y_sc
 ):
     cum = sums_by_token(dt_ref, a_ref)
-    cum_t, dt_t = sums_by_head(dt_ref, a_ref)
+    cum_t, dt_t = sums_by_head(cum), dt_ref[...]
     grow = jnp.exp(cum)
     lower = lower_tri()
     for g in range(2):
@@ -244,9 +262,14 @@
 ):
     at = at_ref[0]
     upper = (at >= 16).astype(jnp.int32)
-    low = jnp.minimum(at, 31 - at)
-    for b in range(33):
+    low = jnp.minimum(at, partner_of(at))
+    high = jnp.maximum(at, partner_of(at))
+
+    def begin(b, none):
         pltpu.make_async_copy(p_hbm.at[b], p_sc.at[b], sem.at[b]).start()
+        return none
+
+    lax.fori_loop(0, low + high + 2, begin, 0)
 
     run = jnp.zeros((SR, T), F32)
     for c in range(31, -1, -1):
@@ -260,7 +283,7 @@
     o_sc[...] = jnp.zeros_like(o_sc)
     dq_sc[...] = jnp.zeros_like(dq_sc)
     for sel in range(2):
-        count = low if sel == 0 else 31 - low
+        count = low if sel == 0 else high
         base = 0 if sel == 0 else low + 1
 
         def first(j, u, delta, sel=sel, base=base):
@@ -314,7 +337,7 @@
     x_ref, b_ref, c_ref, dt_ref, a_ref, skip_ref, dy_ref, r2_ref, gx_ref, gb_ref, gc_ref
 ):
     cum = sums_by_token(dt_ref, a_ref)
-    cum_t, dt_t = sums_by_head(dt_ref, a_ref)
+    cum_t, dt_t = sums_by_head(cum), dt_ref[...]
     grow = jnp.exp(cum)
     lower = lower_tri()
     for g in range(2):
@@ -343,7 +366,7 @@
     x_ref, b_ref, dt_ref, a_ref, gx0_ref, gb0_ref, r5_ref, gx_ref, gb_ref, gk_ref
 ):
     cum = sums_by_token(dt_ref, a_ref)
-    weight = jnp.exp(cum[T - 1 : T, :] - cum) * dt_ref[...]
+    weight = jnp.exp(cum[T - 1 : T, :] - cum) * steps_by_token(dt_ref)
     for g in range(2):
         b = b_ref[:, head(g)]
         gb = gb0_ref[:, head(g)]
@@ -391,8 +414,9 @@
     at1 = at.astype(jnp.int32).reshape(1)
     upper = at >= 16
     a_row = decay_a.reshape(1, NH)
+    steps = step_dt.T
     skip_row = skip_d.reshape(1, NH)
-    swap = [(i, 31 - i) for i in range(32)]
+    swap = [(i, partner_of(i)) for i in range(32)]
 
     away = jnp.concatenate(
         [
@@ -404,46 +428,46 @@
     other = lax.ppermute(away, "ctx", swap)
     (pay1,) = call(
         state_kernel, [((32, SR + DR + T, T), BF)], [], "block_states", 62, 1 << 34, 1 << 22,
-        mamba_x, mamba_b, step_dt, a_row, keys,
+        mamba_x, mamba_b, steps, a_row, keys,
     )
     r1 = over_ctx(pay1)
     pay2, probs, qs, ds = call(
         probs_kernel,
-        [((32, SR + T, T), BF), ((33, T, 1024), F32), ((2, 1024, T), BF), ((2, 1024, T), BF)],
+        [((32, SR + T, T), BF), ((NB, T, 1024), F32), ((2, 1024, T), BF), ((2, 1024, T), BF)],
         [
-            pltpu.VMEM((33, T, 1024), F32), pltpu.VMEM((32, T, T), F32),
+            pltpu.VMEM((NB, T, 1024), F32), pltpu.VMEM((32, T, T), F32),
             pltpu.VMEM((2, T, 1024), BF), pltpu.SemaphoreType.DMA,
         ],
-        "probs", 40, 1 << 32, 1 << 25, at1, r1, queries, out_grad, other, far_out=(1,),
+        "probs", 48, 1 << 32, 1 << 25, at1, r1, queries, out_grad, other, far_out=(1,),
     )
     r2 = over_ctx(pay2)
     (pay3,) = call(
         values_kernel, [((4, T, 512), BF)], [pltpu.VMEM((T, 2048), BF)], "values", 24,
         1 << 30, 1 << 23,
-        mamba_x, mamba_b, mamba_c, step_dt, a_row, skip_row, r2, value_weight,
+        mamba_x, mamba_b, mamba_c, steps, a_row, skip_row, r2, value_weight,
     )
     r3 = lax.all_to_all(pay3, ("ch", "section"), 0, 0, tiled=True)
     pay4, dy = call(
         back_kernel, [((32, SR + T, T), BF), ((T, 2048), F32)], [], "value_back", 24, 1 << 30,
-        1 << 23, r3, value_weight, mamba_c, step_dt, a_row,
+        1 << 23, r3, value_weight, mamba_c, steps, a_row,
     )
     r4 = over_ctx(pay4)
     gx0, gb0, grad_c = call(
         local_kernel,
         [((T, 2048), F32), ((T, 256), F32), ((T, 256), F32)], [], "mixer_local", 24,
         1 << 29, 1 << 23,
-        mamba_x, mamba_b, mamba_c, step_dt, a_row, skip_row, dy, r2,
+        mamba_x, mamba_b, mamba_c, steps, a_row, skip_row, dy, r2,
     )
     pay5, kept, send = call(
         grads_kernel,
         [((32, SR + T, T), BF), ((256, 1024), F32), ((256, 1024), BF)],
         [
-            pltpu.VMEM((33, T, 1024), F32), pltpu.VMEM((33, T, 1024), F32),
+            pltpu.VMEM((NB, T, 1024), F32), pltpu.VMEM((NB, T, 1024), F32),
             pltpu.VMEM((2, T, 1024), F32), pltpu.VMEM((2, T, 1024), F32),
             pltpu.VMEM((32, T, T), F32), pltpu.VMEM((2, T, 1024), BF),
-            pltpu.SemaphoreType.DMA((33,)),
+            pltpu.SemaphoreType.DMA((NB,)),
         ],
-        "attention_grads", 56, 1 << 32, 1 << 25, at1, r1, r4, qs, ds, probs, far_in=(5,),
+        "attention_grads", 62, 1 << 32, 1 << 25, at1, r1, r4, qs, ds, probs, far_in=(5,),
     )
     back = lax.ppermute(send, "ctx", swap)
     r5 = over_ctx(pay5)
@@ -451,7 +475,7 @@
         final_kernel,
         [((T, 2048), F32), ((T, 256), F32), ((T, 256), F32)],
         [], "mixer_grads", 24, 1 << 29, 1 << 23,
-        mamba_x, mamba_b, step_dt, a_row, gx0, gb0, r5,
+        mamba_x, mamba_b, steps, a_row, gx0, gb0, r5,
     )
     back = back.astype(F32)
     whole = jnp.where(

time: 205 us -> 202 us (0.985)
  blocking collectives: 68.2 us -> 75 us
  starting transfers between devices: 30.6 us -> 25.4 us
  Pallas kernels: 44.8 us -> 42.3 us
  local copies, waits for them, and re-layouts: 6.46 us -> 4 us
    all_to_all x2, blocking collectives: 57 us -> 63.7 us  [over_ctx(): return lax.all_to_all(pay, 'ctx', 0, 0, tiled=True)]
    ppermute x1, starting transfers between devices: 7.68 us -> 3.06 us  [body(): back = lax.ppermute(send, 'ctx', swap)]
    ppermute x1, starting transfers between devices: 7.68 us -> 3.12 us  [body(): other = lax.ppermute(away, 'ctx', swap)]
    all_to_all x2, starting transfers between devices: 15.2 us -> 19.2 us  [over_ctx(): return lax.all_to_all(pay, 'ctx', 0, 0, tiled=True)]
    unnamed x39 -> x38, local copies, waits for them, and re-layouts: 5 us -> 2.54 us
    pallas_call x7, Pallas kernels: 44.8 us -> 42.3 us  [call(): pl.pallas_call(kernel, name=name, out_shape=[jax.ShapeDtypeStruct(s, d) f...]
where the time goes in v4:
time: 202 us; the launch traced here: 201 us
  blocking collectives  75 us (37%)
  waiting for transfers between devices  53.3 us (26%)
  Pallas kernels  42.3 us (21%)
  starting transfers between devices  25.4 us (13%)
  local copies, waits for them, and re-layouts  4 us (2%)
    all_to_all x2, blocking collectives, over_ctx(): return lax.all_to_all(pay, 'ctx', 0, 0, tiled=True)  63.7 us
    pallas_call x7, Pallas kernels, call(): pl.pallas_call(kernel, name=name, out_shape=[jax.ShapeDtypeStruct(s, d) f...  42.3 us
    ppermute x1, waiting for transfers between devices, body(): other = lax.ppermute(away, 'ctx', swap)  29.5 us
    ppermute x1, waiting for transfers between devices, body(): back = lax.ppermute(send, 'ctx', swap)  23.8 us
    all_to_all x2, starting transfers between devices, over_ctx(): return lax.all_to_all(pay, 'ctx', 0, 0, tiled=True)  19.2 us
    all_to_all x1, blocking collectives, body(): r3 = lax.all_to_all(pay3, ('ch', 'section'), 0, 0, tiled=True)  11.2 us
  transfers between devices with their start and end apart: 4, of which 2 were waited for; matrix products, arithmetic and copies ran while one was open for 1% of the time, Pallas kernels for 1%

profile of v4, /device:TPU:0, one launch (start us, length us, event | category | flops | bytes accessed | tf_op | source)
XLA Modules:
  0.0 201.4 jit_solution(17377468207680227029)
XLA Ops:
  0.6 3.5 %block_states.1 = bf16[32,208,128]{2,1,0:T(8,128)(2,1)} custom-call(bf16[128,2048]{1,0:T(8,128)(2,1)} %x_ref.7, bf16[128,256]{1,0:T(8,128)(2,1)} %b_ref.7, f32[16,128]{1,0:T(8,128)} %bitcast.4, f32[1,16]{1,0:T(1,128)} %bitcast.9, bf16[128,256]{1,0:T(8,128)(2,1)} %k_ref.1), custom_call_target="tpu_custom_call" | custom-call | flops 17179869184 | bytes 4194304 | tf_op jit(solution)/shard_map/block_states/pallas_call | solution.py:392
  4.1 10.8 %all-to-all-start = ((bf16[32,208,128]{2,1,0:T(8,128)(2,1)}), bf16[32,208,128]{2,1,0:T(8,128)(2,1)S(1)}, u32[]{:S(2)}, u32[]{:S(2)}) async-start(bf16[32,208,128]{2,1,0:T(8,128)(2,1)} %block_states.1), calls=%async_computation | async-start | bytes 3407872 | tf_op jit(solution)/shard_map/all_to_all | solution.py:407
  15.0 0.1 slice_select_fusion
  15.1 3.1 %collective-permute-start = (bf16[256,1024]{1,0:T(8,128)(2,1)S(1)}, bf16[256,1024]{1,0:T(8,128)(2,1)S(1)}, u32[]{:S(2)}, u32[]{:S(2)}) collective-permute-start(bf16[256,1024]{1,0:T(8,128)(2,1)S(1)} %pad_maximum_fusion), channel_id=1, source_target_pairs={{0,96},{4,100},{8,104},{12,108},{16,112},{20,116},{24,120},{28,124... | collective-permute-start | bytes 1572872 | tf_op jit(solution)/shard_map/ppermute | solution.py:428
  18.2 29.5 %collective-permute-done.other_ref = bf16[256,1024]{1,0:T(8,128)(2,1)S(1)} collective-permute-done((bf16[256,1024]{1,0:T(8,128)(2,1)S(1)}, bf16[256,1024]{1,0:T(8,128)(2,1)S(1)}, u32[]{:S(2)}, u32[]{:S(2)}) %collective-permute-start) | collective-permute-done | bytes 524320 | tf_op jit(solution)/shard_map/ppermute | solution.py:428
  47.7 0.0 all-to-all-done.r1_ref
  47.7 11.6 %probs.1 = (bf16[32,192,128]{2,1,0:T(8,128)(2,1)S(1)}, f32[40,128,1024]{2,1,0:T(8,128)}, bf16[2,1024,128]{2,1,0:T(8,128)(2,1)S(1)}, bf16[2,1024,128]{2,1,0:T(8,128)(2,1)S(1)}) custom-call(s32[1]{0:T(128)} %bitcast.at_ref, bf16[32,208,128]{2,1,0:T(8,128)(2,1)S(1)} %all-to-all-done.r1_ref, bf16[128,2048]{1,0:T(8,128)(2,1)S(1)} %copy-done.12, ...), custom_call_target="tpu_custom_call" | custom-call | flops 4294967296 | bytes 33554432 | tf_op jit(solution)/shard_map/probs/pallas_call | solution.py:392
  59.3 0.0 copy-start.10
  59.3 0.0 copy-start.2
  59.4 0.0 copy-start.8
  59.4 0.0 copy-start.9
  59.4 0.0 copy-start.14
  59.4 0.0 copy-start.15
  59.4 0.0 copy-start.16
  59.4 35.5 %all_to_all.25.r2_ref = bf16[32,192,128]{2,1,0:T(8,128)(2,1)S(1)} all-to-all(bf16[32,192,128]{2,1,0:T(8,128)(2,1)S(1)} %get-tuple-element.21), channel_id=1, replica_groups=mesh['ctx'=32,'ch'=2,'section'=2] {'ctx'}, dimensions={0} | all-to-all | bytes 3145728 | tf_op jit(solution)/shard_map/all_to_all | solution.py:407
  95.0 2.2 %values.1 = bf16[4,128,512]{2,1,0:T(8,128)(2,1)S(1)} custom-call(bf16[128,2048]{1,0:T(8,128)(2,1)S(1)} %copy-done.2, bf16[128,256]{1,0:T(8,128)(2,1)S(1)} %copy-done.9, bf16[128,256]{1,0:T(8,128)(2,1)S(1)} %copy-done.8, f32[16,128]{1,0:T(8,128)S(1)} %bitcast.5, f32[1,16]{1,0:T(1,128)S(1)} %bitcast.10, f32[1,16]{1,0:T(1,128)S(1)} %bitcast.14, ...), custom_call_target="tpu_custom_call" | custom-call | flops 1073741824 | bytes 8388608 | tf_op jit(solution)/shard_map/values/pallas_call | solution.py:392
  97.3 11.2 %all_to_all.26.r3_ref = bf16[4,128,512]{2,1,0:T(8,128)(2,1)S(1)} all-to-all(bf16[4,128,512]{2,1,0:T(8,128)(2,1)S(1)} %values.1), channel_id=1, replica_groups=mesh['ctx'=32,'ch'=2,'section'=2] {'ch','section'}, dimensions={0} | all-to-all | bytes 1048576 | tf_op jit(solution)/shard_map/all_to_all | solution.py:449
  108.5 4.0 %value_back.1 = (bf16[32,192,128]{2,1,0:T(8,128)(2,1)S(1)}, f32[128,2048]{1,0:T(8,128)S(1)}) custom-call(bf16[4,128,512]{2,1,0:T(8,128)(2,1)S(1)} %all_to_all.26.r3_ref, bf16[2048,1024]{1,0:T(8,128)(2,1)S(1)} %copy-done, bf16[128,256]{1,0:T(8,128)(2,1)S(1)} %copy-done.8, f32[16,128]{1,0:T(8,128)S(1)} %bitcast.6, f32[1,16]{1,0:T(1,128)S(1)} %bitcast.11), custom_call_target="tpu_custom_call" | custom-call | flops 1073741824 | bytes 8388608 | tf_op jit(solution)/shard_map/value_back/pallas_call | solution.py:392
  112.6 0.0 copy-start.6
  112.6 28.2 %all_to_all.27.r4_ref = bf16[32,192,128]{2,1,0:T(8,128)(2,1)} all-to-all(bf16[32,192,128]{2,1,0:T(8,128)(2,1)S(1)} %get-tuple-element.22), channel_id=1, replica_groups=mesh['ctx'=32,'ch'=2,'section'=2] {'ctx'}, dimensions={0} | all-to-all | bytes 3145728 | tf_op jit(solution)/shard_map/all_to_all | solution.py:407
  140.8 15.2 %attention_grads.1 = (bf16[32,192,128]{2,1,0:T(8,128)(2,1)}, f32[256,1024]{1,0:T(8,128)}, bf16[256,1024]{1,0:T(8,128)(2,1)}) custom-call(s32[1]{0:T(128)} %bitcast.at_ref, bf16[32,208,128]{2,1,0:T(8,128)(2,1)} %copy-done.1, bf16[32,192,128]{2,1,0:T(8,128)(2,1)} %all_to_all.27.r4_ref, bf16[2,1024,128]{2,1,0:T(8,128)(2,1)} %copy-done.10, ...), custom_call_target="tpu_custom_call" | custom-call | flops 4294967296 | bytes 33554432 | tf_op jit(solution)/shard_map/attention_grads/pallas_call | solution.py:392
  156.0 0.0 copy-start.3
  156.0 8.3 %all-to-all-start.4 = ((bf16[32,192,128]{2,1,0:T(8,128)(2,1)}), bf16[32,192,128]{2,1,0:T(8,128)(2,1)}, u32[]{:S(2)}, u32[]{:S(2)}) async-start(bf16[32,192,128]{2,1,0:T(8,128)(2,1)} %get-tuple-element.31), calls=%async_computation.4 | async-start | bytes 3145728 | tf_op jit(solution)/shard_map/all_to_all | solution.py:407
  164.4 3.1 %collective-permute-start.1 = (bf16[256,1024]{1,0:T(8,128)(2,1)S(1)}, bf16[256,1024]{1,0:T(8,128)(2,1)S(1)}, u32[]{:S(2)}, u32[]{:S(2)}) collective-permute-start(bf16[256,1024]{1,0:T(8,128)(2,1)S(1)} %copy-done.18), channel_id=1, source_target_pairs={{0,96},{4,100},{8,104},{12,108},{16,112},{20,116},{24,120},{28,124... | collective-permute-start | bytes 1572872 | tf_op jit(solution)/shard_map/ppermute | solution.py:472
  167.4 1.2 copy-done.7
  168.7 2.6 %mixer_local.1 = (f32[128,2048]{1,0:T(8,128)S(1)}, f32[128,256]{1,0:T(8,128)S(1)}, f32[128,256]{1,0:T(8,128)}) custom-call(bf16[128,2048]{1,0:T(8,128)(2,1)S(1)} %copy-done.3, bf16[128,256]{1,0:T(8,128)(2,1)S(1)} %copy-done.9, bf16[128,256]{1,0:T(8,128)(2,1)S(1)} %copy-done.8, f32[16,128]{1,0:T(8,128)S(1)} %bitcast.7, f32[1,16]{1,0:T(1,128)S(1)} %bitcast.12, ...), custom_call_target="tpu_custom_call" | custom-call | flops 536870912 | bytes 8388608 | tf_op jit(solution)/shard_map/mixer_local/pallas_call | solution.py:392
  171.3 23.8 %collective-permute-done.1 = bf16[256,1024]{1,0:T(8,128)(2,1)S(1)} collective-permute-done((bf16[256,1024]{1,0:T(8,128)(2,1)S(1)}, bf16[256,1024]{1,0:T(8,128)(2,1)S(1)}, u32[]{:S(2)}, u32[]{:S(2)}) %collective-permute-start.1) | collective-permute-done | bytes 524320 | tf_op jit(solution)/shard_map/ppermute | solution.py:472
  195.0 0.1 convert_element_type.3
  195.2 0.3 maximum_select_fusion
  195.5 1.5 fusion
  197.0 1.2 copy-done.5
  198.2 3.2 %mixer_grads.1 = (f32[128,2048]{1,0:T(8,128)}, f32[128,256]{1,0:T(8,128)}, f32[128,256]{1,0:T(8,128)}) custom-call(bf16[128,2048]{1,0:T(8,128)(2,1)S(1)} %copy-done.3, bf16[128,256]{1,0:T(8,128)(2,1)S(1)} %copy-done.9, f32[16,128]{1,0:T(8,128)S(1)} %bitcast.8, f32[1,16]{1,0:T(1,128)S(1)} %bitcast.13, f32[128,2048]{1,0:T(8,128)S(1)} %copy-done.5, ...), custom_call_target="tpu_custom_call" | custom-call | flops 536870912 | bytes 8388608 | tf_op jit(solution)/shard_map/mixer_grads/pallas_call | solution.py:392
  (29 shorter events, 0.1 us)
Async XLA Ops:
  4.1 10.9 %copy-start.12 = (bf16[128,2048]{1,0:T(8,128)(2,1)S(1)}, bf16[128,2048]{1,0:T(8,128)(2,1)}, u32[]{:S(2)}) copy-start(bf16[128,2048]{1,0:T(8,128)(2,1)} %q_ref.1) | copy-start | bytes 1572868
  4.1 10.9 %copy-start.13 = (bf16[128,2048]{1,0:T(8,128)(2,1)S(1)}, bf16[128,2048]{1,0:T(8,128)(2,1)}, u32[]{:S(2)}) copy-start(bf16[128,2048]{1,0:T(8,128)(2,1)} %d_ref.1) | copy-start | bytes 1572868
  4.1 43.6 %all-to-all-start = ((bf16[32,208,128]{2,1,0:T(8,128)(2,1)}), bf16[32,208,128]{2,1,0:T(8,128)(2,1)S(1)}, u32[]{:S(2)}, u32[]{:S(2)}) async-start(bf16[32,208,128]{2,1,0:T(8,128)(2,1)} %block_states.1), calls=%async_computation | async-start | bytes 3407872 | tf_op jit(solution)/shard_map/all_to_all | solution.py:407
  15.1 32.6 %collective-permute-start = (bf16[256,1024]{1,0:T(8,128)(2,1)S(1)}, bf16[256,1024]{1,0:T(8,128)(2,1)S(1)}, u32[]{:S(2)}, u32[]{:S(2)}) collective-permute-start(bf16[256,1024]{1,0:T(8,128)(2,1)S(1)} %pad_maximum_fusion), channel_id=1, source_target_pairs={{0,96},{4,100},{8,104},{12,108},{16,112},{20,116},{24,120},{28,124... | collective-permute-start | bytes 1572872 | tf_op jit(solution)/shard_map/ppermute | solution.py:428
  47.7 11.6 %copy-start.1 = (bf16[32,208,128]{2,1,0:T(8,128)(2,1)}, bf16[32,208,128]{2,1,0:T(8,128)(2,1)S(1)}, u32[]{:S(2)}) copy-start(bf16[32,208,128]{2,1,0:T(8,128)(2,1)S(1)} %all-to-all-done.r1_ref) | copy-start | bytes 5111812
  47.7 47.2 %copy-start = (bf16[2048,1024]{1,0:T(8,128)(2,1)S(1)}, bf16[2048,1024]{1,0:T(8,128)(2,1)}, u32[]{:S(2)}) copy-start(bf16[2048,1024]{1,0:T(8,128)(2,1)} %w_ref.3) | copy-start | bytes 12582916
  59.3 37.9 %copy-start.10 = (bf16[2,1024,128]{2,1,0:T(8,128)(2,1)}, bf16[2,1024,128]{2,1,0:T(8,128)(2,1)S(1)}, u32[]{:S(2)}) copy-start(bf16[2,1024,128]{2,1,0:T(8,128)(2,1)S(1)} %get-tuple-element.23.qs_ref) | copy-start | bytes 1572868
  59.3 37.9 %copy-start.11 = (bf16[2,1024,128]{2,1,0:T(8,128)(2,1)}, bf16[2,1024,128]{2,1,0:T(8,128)(2,1)S(1)}, u32[]{:S(2)}) copy-start(bf16[2,1024,128]{2,1,0:T(8,128)(2,1)S(1)} %get-tuple-element.24.ds_ref) | copy-start | bytes 1572868
  59.3 35.6 %copy-start.2 = (bf16[128,2048]{1,0:T(8,128)(2,1)S(1)}, bf16[128,2048]{1,0:T(8,128)(2,1)}, u32[]{:S(2)}) copy-start(bf16[128,2048]{1,0:T(8,128)(2,1)} %x_ref.7) | copy-start | bytes 1572868
  59.4 35.6 %copy-start.8 = (bf16[128,256]{1,0:T(8,128)(2,1)S(1)}, bf16[128,256]{1,0:T(8,128)(2,1)}, u32[]{:S(2)}) copy-start(bf16[128,256]{1,0:T(8,128)(2,1)} %c_ref.5) | copy-start | bytes 196612
  59.4 35.6 %copy-start.9 = (bf16[128,256]{1,0:T(8,128)(2,1)S(1)}, bf16[128,256]{1,0:T(8,128)(2,1)}, u32[]{:S(2)}) copy-start(bf16[128,256]{1,0:T(8,128)(2,1)} %b_ref.7) | copy-start | bytes 196612
  59.4 35.6 %copy-start.14 = (f32[128,16]{0,1:T(8,128)S(1)}, f32[128,16]{0,1:T(8,128)}, u32[]{:S(2)}) copy-start(f32[128,16]{0,1:T(8,128)} %param.13) | copy-start | bytes 24580
  59.4 35.6 %copy-start.15 = (f32[16]{0:T(128)S(1)}, f32[16]{0:T(128)}, u32[]{:S(2)}) copy-start(f32[16]{0:T(128)} %param.14) | copy-start | bytes 196
  59.4 35.6 %copy-start.16 = (f32[16]{0:T(128)S(1)}, f32[16]{0:T(128)}, u32[]{:S(2)}) copy-start(f32[16]{0:T(128)} %param.15) | copy-start | bytes 196
  112.6 28.2 %copy-start.6 = (f32[128,2048]{1,0:T(8,128)}, f32[128,2048]{1,0:T(8,128)S(1)}, u32[]{:S(2)}) copy-start(f32[128,2048]{1,0:T(8,128)S(1)} %get-tuple-element.28.dy_ref) | copy-start | bytes 3145732
  156.0 8.4 %copy-start.18 = (bf16[256,1024]{1,0:T(8,128)(2,1)S(1)}, bf16[256,1024]{1,0:T(8,128)(2,1)}, u32[]{:S(2)}) copy-start(bf16[256,1024]{1,0:T(8,128)(2,1)} %get-tuple-element.26) | copy-start | bytes 1572868
  156.0 11.4 %copy-start.3 = (bf16[128,2048]{1,0:T(8,128)(2,1)S(1)}, bf16[128,2048]{1,0:T(8,128)(2,1)}, u32[]{:S(2)}) copy-start(bf16[128,2048]{1,0:T(8,128)(2,1)} %x_ref.7) | copy-start | bytes 1572868
  156.0 41.0 %all-to-all-start.4 = ((bf16[32,192,128]{2,1,0:T(8,128)(2,1)}), bf16[32,192,128]{2,1,0:T(8,128)(2,1)}, u32[]{:S(2)}, u32[]{:S(2)}) async-start(bf16[32,192,128]{2,1,0:T(8,128)(2,1)} %get-tuple-element.31), calls=%async_computation.4 | async-start | bytes 3145728 | tf_op jit(solution)/shard_map/all_to_all | solution.py:407
  164.4 30.7 %collective-permute-start.1 = (bf16[256,1024]{1,0:T(8,128)(2,1)S(1)}, bf16[256,1024]{1,0:T(8,128)(2,1)S(1)}, u32[]{:S(2)}, u32[]{:S(2)}) collective-permute-start(bf16[256,1024]{1,0:T(8,128)(2,1)S(1)} %copy-done.18), channel_id=1, source_target_pairs={{0,96},{4,100},{8,104},{12,108},{16,112},{20,116},{24,120},{28,124... | collective-permute-start | bytes 1572872 | tf_op jit(solution)/shard_map/ppermute | solution.py:472
  167.4 1.2 copy-start.7
  168.7 26.5 %copy-start.17 = (f32[256,1024]{1,0:T(8,128)S(1)}, f32[256,1024]{1,0:T(8,128)}, u32[]{:S(2)}) copy-start(f32[256,1024]{1,0:T(8,128)} %get-tuple-element.27) | copy-start | bytes 3145732
  171.3 24.2 %copy-start.4 = (f32[128,2048]{1,0:T(8,128)}, f32[128,2048]{1,0:T(8,128)S(1)}, u32[]{:S(2)}) copy-start(f32[128,2048]{1,0:T(8,128)S(1)} %get-tuple-element.29.gx0_ref) | copy-start | bytes 3145732
  197.0 1.2 copy-start.5

commit v5 on v4

--- a/solution.py
+++ b/solution.py
@@ -52,8 +52,10 @@
     return -mm_exact(lower_tri().astype(F32), dt_ref[...], NT) * a_ref[...]
 
 
-def steps_by_token(dt_ref):
-    return mm_exact(same_token(), dt_ref[...], NT)
+def sums_and_steps(dt_ref, a_ref):
+    picks = jnp.concatenate([lower_tri().astype(F32), same_token()], axis=0)
+    both = mm_exact(picks, dt_ref[...], NT)
+    return -both[:T] * a_ref[...], both[T:]
 
 
 def sums_by_head(cum):
@@ -61,9 +63,9 @@
 
 
 def state_kernel(x_ref, b_ref, dt_ref, a_ref, k_ref, out_ref):
-    cum = sums_by_token(dt_ref, a_ref)
+    cum, steps = sums_and_steps(dt_ref, a_ref)
     total = cum[T - 1 : T, :]
-    weight = jnp.exp(total - cum) * steps_by_token(dt_ref)
+    weight = jnp.exp(total - cum) * steps
     first = total.astype(BF).astype(F32)
     second = (total - first).astype(BF).astype(F32)
     third = total - first - second
@@ -334,9 +336,11 @@
 
 
 def local_kernel(
-    x_ref, b_ref, c_ref, dt_ref, a_ref, skip_ref, dy_ref, r2_ref, gx_ref, gb_ref, gc_ref
+    x_ref, b_ref, c_ref, dt_ref, a_ref, skip_ref, dy_ref, r2_ref, gx_ref, gb_ref, gc_ref,
+    weight_ref
 ):
-    cum = sums_by_token(dt_ref, a_ref)
+    cum, steps = sums_and_steps(dt_ref, a_ref)
+    weight_ref[...] = jnp.exp(cum[T - 1 : T, :] - cum) * steps
     cum_t, dt_t = sums_by_head(cum), dt_ref[...]
     grow = jnp.exp(cum)
     lower = lower_tri()
@@ -363,10 +367,9 @@
 
 
 def final_kernel(
-    x_ref, b_ref, dt_ref, a_ref, gx0_ref, gb0_ref, r5_ref, gx_ref, gb_ref, gk_ref
+    x_ref, b_ref, weight_ref, gx0_ref, gb0_ref, r5_ref, gx_ref, gb_ref, gk_ref
 ):
-    cum = sums_by_token(dt_ref, a_ref)
-    weight = jnp.exp(cum[T - 1 : T, :] - cum) * steps_by_token(dt_ref)
+    weight = weight_ref[...]
     for g in range(2):
         b = b_ref[:, head(g)]
         gb = gb0_ref[:, head(g)]
@@ -452,9 +455,9 @@
         1 << 23, r3, value_weight, mamba_c, steps, a_row,
     )
     r4 = over_ctx(pay4)
-    gx0, gb0, grad_c = call(
+    gx0, gb0, grad_c, weight = call(
         local_kernel,
-        [((T, 2048), F32), ((T, 256), F32), ((T, 256), F32)], [], "mixer_local", 24,
+        [((T, 2048), F32), ((T, 256), F32), ((T, 256), F32), ((T, NH), F32)], [], "mixer_local", 24,
         1 << 29, 1 << 23,
         mamba_x, mamba_b, mamba_c, steps, a_row, skip_row, dy, r2,
     )
@@ -475,13 +478,20 @@
         final_kernel,
         [((T, 2048), F32), ((T, 256), F32), ((T, 256), F32)],
         [], "mixer_grads", 24, 1 << 29, 1 << 23,
-        mamba_x, mamba_b, steps, a_row, gx0, gb0, r5,
-    )
-    back = back.astype(F32)
-    whole = jnp.where(
-        upper, jnp.concatenate([back, kept], axis=1), jnp.concatenate([kept, back], axis=1)
-    )
-    return (whole[:T], whole[T:], grad_k, grad_x, grad_b, grad_c)
+        mamba_x, mamba_b, weight, gx0, gb0, r5,
+    )
+    kept, grad_k = lax.optimization_barrier((kept, grad_k))
+
+    def joined(first):
+        mine = kept[first : first + T]
+        theirs = back[first : first + T].astype(F32)
+        return jnp.where(
+            upper,
+            jnp.concatenate([theirs, mine], axis=1),
+            jnp.concatenate([mine, theirs], axis=1),
+        )
+
+    return (joined(0), joined(T), grad_k, grad_x, grad_b, grad_c)
 
 
 def solution(mesh):

time: 202 us -> 201 us (level)
  transfers between devices with their start and end apart: 4 -> 4, of which waited for: 2 -> 2; matrix products, arithmetic and copies ran while one was open for 1% -> 0% of each run, Pallas kernels for 1% -> 1%
where the time goes in v5:
time: 201 us
  blocking collectives  74.9 us (37%)
  waiting for transfers between devices  52.2 us (26%)
  Pallas kernels  42.1 us (21%)
  starting transfers between devices  25.2 us (13%)
  local copies, waits for them, and re-layouts  3.48 us (2%)
    all_to_all x2, blocking collectives, over_ctx(): return lax.all_to_all(pay, 'ctx', 0, 0, tiled=True)  63.7 us
    pallas_call x7, Pallas kernels, call(): pl.pallas_call(kernel, name=name, out_shape=[jax.ShapeDtypeStruct(s, d) f...  42.1 us
    ppermute x1, waiting for transfers between devices, body(): other = lax.ppermute(away, 'ctx', swap)  29.5 us
    ppermute x1, waiting for transfers between devices, body(): back = lax.ppermute(send, 'ctx', swap)  22.7 us
    all_to_all x2, starting transfers between devices, over_ctx(): return lax.all_to_all(pay, 'ctx', 0, 0, tiled=True)  19 us
    all_to_all x1, blocking collectives, body(): r3 = lax.all_to_all(pay3, ('ch', 'section'), 0, 0, tiled=True)  11.2 us
  transfers between devices with their start and end apart: 4, of which 2 were waited for; matrix products, arithmetic and copies ran while one was open for 0% of the time, Pallas kernels for 1%

profile of v5, /device:TPU:0, one launch (start us, length us, event | category | flops | bytes accessed | tf_op | source)
XLA Modules:
  0.0 200.6 jit_solution(11395379419740428523)
XLA Ops:
  0.6 3.5 %block_states.1 = bf16[32,208,128]{2,1,0:T(8,128)(2,1)} custom-call(bf16[128,2048]{1,0:T(8,128)(2,1)} %x_ref.7, bf16[128,256]{1,0:T(8,128)(2,1)} %b_ref.7, f32[16,128]{1,0:T(8,128)} %bitcast.4, f32[1,16]{1,0:T(1,128)} %bitcast.8, bf16[128,256]{1,0:T(8,128)(2,1)} %k_ref.1), custom_call_target="tpu_custom_call" | custom-call | flops 17179869184 | bytes 4194304 | tf_op jit(solution)/shard_map/block_states/pallas_call | solution.py:395
  4.1 10.8 %all-to-all-start = ((bf16[32,208,128]{2,1,0:T(8,128)(2,1)}), bf16[32,208,128]{2,1,0:T(8,128)(2,1)S(1)}, u32[]{:S(2)}, u32[]{:S(2)}) async-start(bf16[32,208,128]{2,1,0:T(8,128)(2,1)} %block_states.1), calls=%async_computation | async-start | bytes 3407872 | tf_op jit(solution)/shard_map/all_to_all | solution.py:410
  15.1 3.1 %collective-permute-start = (bf16[256,1024]{1,0:T(8,128)(2,1)S(1)}, bf16[256,1024]{1,0:T(8,128)(2,1)S(1)}, u32[]{:S(2)}, u32[]{:S(2)}) collective-permute-start(bf16[256,1024]{1,0:T(8,128)(2,1)S(1)} %pad_maximum_fusion), channel_id=1, source_target_pairs={{0,96},{4,100},{8,104},{12,108},{16,112},{20,116},{24,120},{28,124... | collective-permute-start | bytes 1572872 | tf_op jit(solution)/shard_map/ppermute | solution.py:431
  18.2 29.5 %collective-permute-done.other_ref = bf16[256,1024]{1,0:T(8,128)(2,1)S(1)} collective-permute-done((bf16[256,1024]{1,0:T(8,128)(2,1)S(1)}, bf16[256,1024]{1,0:T(8,128)(2,1)S(1)}, u32[]{:S(2)}, u32[]{:S(2)}) %collective-permute-start) | collective-permute-done | bytes 524320 | tf_op jit(solution)/shard_map/ppermute | solution.py:431
  47.7 11.5 %probs.1 = (bf16[32,192,128]{2,1,0:T(8,128)(2,1)S(1)}, f32[40,128,1024]{2,1,0:T(8,128)}, bf16[2,1024,128]{2,1,0:T(8,128)(2,1)S(1)}, bf16[2,1024,128]{2,1,0:T(8,128)(2,1)S(1)}) custom-call(s32[1]{0:T(128)} %bitcast.at_ref, bf16[32,208,128]{2,1,0:T(8,128)(2,1)S(1)} %all-to-all-done.r1_ref, bf16[128,2048]{1,0:T(8,128)(2,1)S(1)} %copy-done.12, ...), custom_call_target="tpu_custom_call" | custom-call | flops 4294967296 | bytes 33554432 | tf_op jit(solution)/shard_map/probs/pallas_call | solution.py:395
  59.3 0.0 copy-start.10
  59.3 0.0 copy-start.2
  59.3 0.0 copy-start.8
  59.3 0.0 copy-start.9
  59.4 0.0 copy-start.14
  59.4 0.0 copy-start.15
  59.4 0.0 copy-start.16
  59.4 35.5 %all_to_all.25.r2_ref = bf16[32,192,128]{2,1,0:T(8,128)(2,1)S(1)} all-to-all(bf16[32,192,128]{2,1,0:T(8,128)(2,1)S(1)} %get-tuple-element.24), channel_id=1, replica_groups=mesh['ctx'=32,'ch'=2,'section'=2] {'ctx'}, dimensions={0} | all-to-all | bytes 3145728 | tf_op jit(solution)/shard_map/all_to_all | solution.py:410
  94.9 2.1 %values.1 = bf16[4,128,512]{2,1,0:T(8,128)(2,1)S(1)} custom-call(bf16[128,2048]{1,0:T(8,128)(2,1)S(1)} %copy-done.2, bf16[128,256]{1,0:T(8,128)(2,1)S(1)} %copy-done.9, bf16[128,256]{1,0:T(8,128)(2,1)S(1)} %copy-done.8, f32[16,128]{1,0:T(8,128)S(1)} %bitcast.5, f32[1,16]{1,0:T(1,128)S(1)} %bitcast.9, f32[1,16]{1,0:T(1,128)S(1)} %bitcast.12, ...), custom_call_target="tpu_custom_call" | custom-call | flops 1073741824 | bytes 8388608 | tf_op jit(solution)/shard_map/values/pallas_call | solution.py:395
  97.1 11.2 %all_to_all.26.r3_ref = bf16[4,128,512]{2,1,0:T(8,128)(2,1)S(1)} all-to-all(bf16[4,128,512]{2,1,0:T(8,128)(2,1)S(1)} %values.1), channel_id=1, replica_groups=mesh['ctx'=32,'ch'=2,'section'=2] {'ch','section'}, dimensions={0} | all-to-all | bytes 1048576 | tf_op jit(solution)/shard_map/all_to_all | solution.py:452
  108.3 4.0 %value_back.1 = (bf16[32,192,128]{2,1,0:T(8,128)(2,1)S(1)}, f32[128,2048]{1,0:T(8,128)S(1)}) custom-call(bf16[4,128,512]{2,1,0:T(8,128)(2,1)S(1)} %all_to_all.26.r3_ref, bf16[2048,1024]{1,0:T(8,128)(2,1)S(1)} %copy-done, bf16[128,256]{1,0:T(8,128)(2,1)S(1)} %copy-done.8, f32[16,128]{1,0:T(8,128)S(1)} %bitcast.6, f32[1,16]{1,0:T(1,128)S(1)} %bitcast.10), custom_call_target="tpu_custom_call" | custom-call | flops 1073741824 | bytes 8388608 | tf_op jit(solution)/shard_map/value_back/pallas_call | solution.py:395
  112.4 0.0 copy-start.4
  112.4 28.2 %all_to_all.27.r4_ref = bf16[32,192,128]{2,1,0:T(8,128)(2,1)} all-to-all(bf16[32,192,128]{2,1,0:T(8,128)(2,1)S(1)} %get-tuple-element.25), channel_id=1, replica_groups=mesh['ctx'=32,'ch'=2,'section'=2] {'ctx'}, dimensions={0} | all-to-all | bytes 3145728 | tf_op jit(solution)/shard_map/all_to_all | solution.py:410
  140.6 15.1 %attention_grads.1 = (bf16[32,192,128]{2,1,0:T(8,128)(2,1)}, f32[256,1024]{1,0:T(8,128)}, bf16[256,1024]{1,0:T(8,128)(2,1)}) custom-call(s32[1]{0:T(128)} %bitcast.at_ref, bf16[32,208,128]{2,1,0:T(8,128)(2,1)} %copy-done.1, bf16[32,192,128]{2,1,0:T(8,128)(2,1)} %all_to_all.27.r4_ref, bf16[2,1024,128]{2,1,0:T(8,128)(2,1)} %copy-done.10, ...), custom_call_target="tpu_custom_call" | custom-call | flops 4294967296 | bytes 33554432 | tf_op jit(solution)/shard_map/attention_grads/pallas_call | solution.py:395
  155.7 0.0 copy-start.3
  155.7 8.1 %all-to-all-start.4 = ((bf16[32,192,128]{2,1,0:T(8,128)(2,1)}), bf16[32,192,128]{2,1,0:T(8,128)(2,1)}, u32[]{:S(2)}, u32[]{:S(2)}) async-start(bf16[32,192,128]{2,1,0:T(8,128)(2,1)} %get-tuple-element.35), calls=%async_computation.4 | async-start | bytes 3145728 | tf_op jit(solution)/shard_map/all_to_all | solution.py:410
  163.9 3.1 %collective-permute-start.1 = (bf16[256,1024]{1,0:T(8,128)(2,1)S(1)}, bf16[256,1024]{1,0:T(8,128)(2,1)S(1)}, u32[]{:S(2)}, u32[]{:S(2)}) collective-permute-start(bf16[256,1024]{1,0:T(8,128)(2,1)S(1)} %copy-done.18), channel_id=1, source_target_pairs={{0,96},{4,100},{8,104},{12,108},{16,112},{20,116},{24,120},{28,124... | collective-permute-start | bytes 1572872 | tf_op jit(solution)/shard_map/ppermute | solution.py:475
  167.0 1.2 copy-done.5
  168.2 2.7 %mixer_local.1 = (f32[128,2048]{1,0:T(8,128)S(1)}, f32[128,256]{1,0:T(8,128)S(1)}, f32[128,256]{1,0:T(8,128)}, f32[128,16]{1,0:T(8,128)S(1)}) custom-call(bf16[128,2048]{1,0:T(8,128)(2,1)S(1)} %copy-done.3, bf16[128,256]{1,0:T(8,128)(2,1)S(1)} %copy-done.9, bf16[128,256]{1,0:T(8,128)(2,1)S(1)} %copy-done.8, f32[16,128]{1,0:T(8,128)S(1)} %bitcast.7, ...), custom_call_target="tpu_custom_call" | custom-call | flops 536870912 | bytes 8388608 | tf_op jit(solution)/shard_map/mixer_local/pallas_call | solution.py:395
  170.9 1.0 copy-done.6
  171.9 22.7 %collective-permute-done.1 = bf16[256,1024]{1,0:T(8,128)(2,1)S(1)} collective-permute-done((bf16[256,1024]{1,0:T(8,128)(2,1)S(1)}, bf16[256,1024]{1,0:T(8,128)(2,1)S(1)}, u32[]{:S(2)}, u32[]{:S(2)}) %collective-permute-start.1) | collective-permute-done | bytes 524320 | tf_op jit(solution)/shard_map/ppermute | solution.py:475
  194.6 0.1 slice_convert_fusion
  194.7 0.0 all-to-all-done.4.r5_ref
  194.7 1.1 copy-done.7
  195.8 3.1 %mixer_grads.1 = (f32[128,2048]{1,0:T(8,128)}, f32[128,256]{1,0:T(8,128)}, f32[128,256]{1,0:T(8,128)}) custom-call(bf16[128,2048]{1,0:T(8,128)(2,1)S(1)} %copy-done.3, bf16[128,256]{1,0:T(8,128)(2,1)S(1)} %copy-done.9, f32[128,16]{1,0:T(8,128)S(1)} %get-tuple-element.32.weight_ref, f32[128,2048]{1,0:T(8,128)S(1)} %copy-done.7, ...), custom_call_target="tpu_custom_call" | custom-call | flops 536870912 | bytes 8388608 | tf_op jit(solution)/shard_map/mixer_grads/pallas_call | solution.py:395
  198.9 0.1 fusion
  199.0 1.6 maximum_select_fusion
  (30 shorter events, 0.2 us)
Async XLA Ops:
  4.1 10.9 %copy-start.12 = (bf16[128,2048]{1,0:T(8,128)(2,1)S(1)}, bf16[128,2048]{1,0:T(8,128)(2,1)}, u32[]{:S(2)}) copy-start(bf16[128,2048]{1,0:T(8,128)(2,1)} %q_ref.1) | copy-start | bytes 1572868
  4.1 10.9 %copy-start.13 = (bf16[128,2048]{1,0:T(8,128)(2,1)S(1)}, bf16[128,2048]{1,0:T(8,128)(2,1)}, u32[]{:S(2)}) copy-start(bf16[128,2048]{1,0:T(8,128)(2,1)} %d_ref.1) | copy-start | bytes 1572868
  4.1 43.6 %all-to-all-start = ((bf16[32,208,128]{2,1,0:T(8,128)(2,1)}), bf16[32,208,128]{2,1,0:T(8,128)(2,1)S(1)}, u32[]{:S(2)}, u32[]{:S(2)}) async-start(bf16[32,208,128]{2,1,0:T(8,128)(2,1)} %block_states.1), calls=%async_computation | async-start | bytes 3407872 | tf_op jit(solution)/shard_map/all_to_all | solution.py:410
  15.1 32.6 %collective-permute-start = (bf16[256,1024]{1,0:T(8,128)(2,1)S(1)}, bf16[256,1024]{1,0:T(8,128)(2,1)S(1)}, u32[]{:S(2)}, u32[]{:S(2)}) collective-permute-start(bf16[256,1024]{1,0:T(8,128)(2,1)S(1)} %pad_maximum_fusion), channel_id=1, source_target_pairs={{0,96},{4,100},{8,104},{12,108},{16,112},{20,116},{24,120},{28,124... | collective-permute-start | bytes 1572872 | tf_op jit(solution)/shard_map/ppermute | solution.py:431
  47.7 11.6 %copy-start.1 = (bf16[32,208,128]{2,1,0:T(8,128)(2,1)}, bf16[32,208,128]{2,1,0:T(8,128)(2,1)S(1)}, u32[]{:S(2)}) copy-start(bf16[32,208,128]{2,1,0:T(8,128)(2,1)S(1)} %all-to-all-done.r1_ref) | copy-start | bytes 5111812
  47.7 47.1 %copy-start = (bf16[2048,1024]{1,0:T(8,128)(2,1)S(1)}, bf16[2048,1024]{1,0:T(8,128)(2,1)}, u32[]{:S(2)}) copy-start(bf16[2048,1024]{1,0:T(8,128)(2,1)} %w_ref.3) | copy-start | bytes 12582916
  59.3 35.6 %copy-start.10 = (bf16[2,1024,128]{2,1,0:T(8,128)(2,1)}, bf16[2,1024,128]{2,1,0:T(8,128)(2,1)S(1)}, u32[]{:S(2)}) copy-start(bf16[2,1024,128]{2,1,0:T(8,128)(2,1)S(1)} %get-tuple-element.26.qs_ref) | copy-start | bytes 1572868
  59.3 35.6 %copy-start.11 = (bf16[2,1024,128]{2,1,0:T(8,128)(2,1)}, bf16[2,1024,128]{2,1,0:T(8,128)(2,1)S(1)}, u32[]{:S(2)}) copy-start(bf16[2,1024,128]{2,1,0:T(8,128)(2,1)S(1)} %get-tuple-element.27.ds_ref) | copy-start | bytes 1572868
  59.3 35.6 %copy-start.2 = (bf16[128,2048]{1,0:T(8,128)(2,1)S(1)}, bf16[128,2048]{1,0:T(8,128)(2,1)}, u32[]{:S(2)}) copy-start(bf16[128,2048]{1,0:T(8,128)(2,1)} %x_ref.7) | copy-start | bytes 1572868
  59.3 35.6 %copy-start.8 = (bf16[128,256]{1,0:T(8,128)(2,1)S(1)}, bf16[128,256]{1,0:T(8,128)(2,1)}, u32[]{:S(2)}) copy-start(bf16[128,256]{1,0:T(8,128)(2,1)} %c_ref.5) | copy-start | bytes 196612
  59.3 35.6 %copy-start.9 = (bf16[128,256]{1,0:T(8,128)(2,1)S(1)}, bf16[128,256]{1,0:T(8,128)(2,1)}, u32[]{:S(2)}) copy-start(bf16[128,256]{1,0:T(8,128)(2,1)} %b_ref.7) | copy-start | bytes 196612
  59.4 35.6 %copy-start.14 = (f32[128,16]{0,1:T(8,128)S(1)}, f32[128,16]{0,1:T(8,128)}, u32[]{:S(2)}) copy-start(f32[128,16]{0,1:T(8,128)} %param.13) | copy-start | bytes 24580
  59.4 35.6 %copy-start.15 = (f32[16]{0:T(128)S(1)}, f32[16]{0:T(128)}, u32[]{:S(2)}) copy-start(f32[16]{0:T(128)} %param.14) | copy-start | bytes 196
  59.4 35.6 %copy-start.16 = (f32[16]{0:T(128)S(1)}, f32[16]{0:T(128)}, u32[]{:S(2)}) copy-start(f32[16]{0:T(128)} %param.15) | copy-start | bytes 196
  112.4 28.2 %copy-start.4 = (f32[128,2048]{1,0:T(8,128)}, f32[128,2048]{1,0:T(8,128)S(1)}, u32[]{:S(2)}) copy-start(f32[128,2048]{1,0:T(8,128)S(1)} %get-tuple-element.31.dy_ref) | copy-start | bytes 3145732
  155.7 8.2 %copy-start.18 = (bf16[256,1024]{1,0:T(8,128)(2,1)S(1)}, bf16[256,1024]{1,0:T(8,128)(2,1)}, u32[]{:S(2)}) copy-start(bf16[256,1024]{1,0:T(8,128)(2,1)} %get-tuple-element.29) | copy-start | bytes 1572868
  155.7 11.2 %copy-start.3 = (bf16[128,2048]{1,0:T(8,128)(2,1)S(1)}, bf16[128,2048]{1,0:T(8,128)(2,1)}, u32[]{:S(2)}) copy-start(bf16[128,2048]{1,0:T(8,128)(2,1)} %x_ref.7) | copy-start | bytes 1572868
  155.7 38.9 %all-to-all-start.4 = ((bf16[32,192,128]{2,1,0:T(8,128)(2,1)}), bf16[32,192,128]{2,1,0:T(8,128)(2,1)}, u32[]{:S(2)}, u32[]{:S(2)}) async-start(bf16[32,192,128]{2,1,0:T(8,128)(2,1)} %get-tuple-element.35), calls=%async_computation.4 | async-start | bytes 3145728 | tf_op jit(solution)/shard_map/all_to_all | solution.py:410
  163.9 30.7 %collective-permute-start.1 = (bf16[256,1024]{1,0:T(8,128)(2,1)S(1)}, bf16[256,1024]{1,0:T(8,128)(2,1)S(1)}, u32[]{:S(2)}, u32[]{:S(2)}) collective-permute-start(bf16[256,1024]{1,0:T(8,128)(2,1)S(1)} %copy-done.18), channel_id=1, source_target_pairs={{0,96},{4,100},{8,104},{12,108},{16,112},{20,116},{24,120},{28,124... | collective-permute-start | bytes 1572872 | tf_op jit(solution)/shard_map/ppermute | solution.py:475
  167.0 1.2 copy-start.5
  170.9 1.0 copy-start.6
  194.6 1.2 copy-start.7
  195.8 3.1 %copy-start.17 = (f32[256,1024]{1,0:T(8,128)S(1)}, f32[256,1024]{1,0:T(8,128)}, u32[]{:S(2)}) copy-start(f32[256,1024]{1,0:T(8,128)} %get-tuple-element.37) | copy-start | bytes 3145732
